TPU v7x, 128 devices: a whole 4x4x4 slice. The times are simulated.
128 devices in a mesh: sub: 16 (over z, x), grp: 8 (over y, core).
Axes of the slice: x: 4, y: 4, z: 4, core: 2. Of those that a mesh axis runs over, the one named last changes fastest.
Arguments:
- rhs: float32 [8, 64, 256, 256], P('grp', 'sub')
- counts: int32 [8, 64], P('grp', 'sub'), may hold values from 64 to 256, as said below
- solve_panel: bfloat16 [8, 64, 512, 512], P('grp', 'sub'), as said below
- dirichlet_panel: bfloat16 [8, 64, 512, 512], P('grp', 'sub'), as said below
- coupling: float32 [8, 64, 32, 512], P('grp', 'sub'), may hold values from -0.25 to 0.25
- corner_map: int32 [8, 64, 32], P('grp', 'sub'), may hold values from 0 to 2047
- coarse_inverse: float32 [16, 2048, 2048], P('sub', 'grp'), as said below
Outputs:
- multipliers: float32 [8, 64, 256, 256], P('grp', 'sub')
- residual: float32 [8, 64, 256, 256], P('grp', 'sub')
Inputs may be any that keep to these rules, and one draw needn't show every extreme that they name: `counts`: some pair has all 256 unknowns constrained. `solve_panel`: each panel is symmetric positive definite. `dirichlet_panel`: each panel is symmetric positive definite. `coarse_inverse`: each slab's matrix is symmetric positive definite.
All inputs are finite; a program needn't handle non-finite values.
Results may differ from a plain program's by a relative error of at most 0.0003.
Values sent between devices are 32-bit elements; how exact they have to be, the bound alone decides.
A program may use at most 128 MiB of HBM per device.

v0:
```python
import jax
import jax.numpy as jnp
from jax import lax
from jax.sharding import PartitionSpec as P

ITERS = 3


HIGH = lax.Precision.HIGHEST


def passed_along(block, axis, distance):
    devices = range(lax.axis_size(axis))
    route = [(i - distance, i) for i in devices if i - distance in devices]
    return lax.ppermute(block, axis, route)


def spread_faces(values):
    previous = passed_along(values[:, -1:], "sub", 1)
    prior = jnp.concatenate([previous, values[:, :-1]], axis=1)
    return jnp.concatenate([-prior, values], axis=3)


def face_jump(result, live_mask):
    width = result.shape[3] // 2
    following = passed_along(result[:, :1, :, :width], "sub", -1)
    next_left = jnp.concatenate([result[:, 1:, :, :width], following], axis=1)
    return live_mask * (result[..., width:] - next_left)


def panel_apply(panel, face_vals):
    return jnp.einsum(
        "gsrp,gsqp->gsrq", face_vals, panel, precision=HIGH, preferred_element_type=jnp.float32
    )


def inner(first, second):
    return jnp.sum(first * second, axis=(0, 1, 3))


def expand(scalars):
    return scalars[None, None, :, None]


def residual_sum(resid, precond):
    return lax.psum(inner(resid, precond), ("sub", "grp"))


def local(rhs, counts, solve_panel, dirichlet_panel, coupling, corner_map, coarse_inverse):
    local_subs = rhs.shape[1]
    width = rhs.shape[3]
    size = coarse_inverse.shape[2]
    last_device = lax.axis_index("sub") == lax.axis_size("sub") - 1
    slots = jnp.arange(local_subs, dtype=jnp.int32)
    positions = jnp.arange(width, dtype=jnp.int32)
    not_last = jnp.logical_not(last_device & (slots == local_subs - 1))
    live = (positions[None, None, :] < counts[:, :, None]) & not_last[None, :, None]
    live_mask = live.astype(jnp.float32)[:, :, None, :]
    corner_onehot = (corner_map[0][..., None] == jnp.arange(size, dtype=jnp.int32)).astype(
        jnp.float32
    )

    def precondition(values):
        return 0.25 * face_jump(panel_apply(dirichlet_panel, spread_faces(values)), live_mask)

    multipliers = jnp.zeros_like(rhs)
    residual = live_mask * rhs
    precond = precondition(residual)
    direction = precond
    rz_now = residual_sum(residual, precond)
    for step in range(ITERS):
        apply_face_vals = spread_faces(direction)
        corner_vals = jnp.einsum("srp,skp->srk", apply_face_vals[0], coupling[0], precision=HIGH)
        owned_totals = lax.psum_scatter(
            jnp.einsum("skn,srk->nr", corner_onehot, corner_vals, precision=HIGH),
            "grp",
            scatter_dimension=0,
            tiled=True,
        )
        partial_solved = jnp.einsum("mn,mr->nr", coarse_inverse[0], owned_totals, precision=HIGH)
        solved = lax.psum(partial_solved, "grp")
        back = jnp.einsum("skn,nr->srk", corner_onehot, solved, precision=HIGH)
        result = (
            panel_apply(solve_panel, apply_face_vals)
            + jnp.einsum("srk,skp->srp", back, coupling[0], precision=HIGH)[None]
        )
        image = face_jump(result, live_mask)
        alpha = rz_now / lax.psum(inner(direction, image), ("sub", "grp"))
        multipliers = multipliers + expand(alpha) * direction
        residual = residual - expand(alpha) * image
        if step + 1 < ITERS:
            precond = precondition(residual)
            rz_next = residual_sum(residual, precond)
            direction = precond + expand(rz_next / rz_now) * direction
            rz_now = rz_next
    return (multipliers, residual)


def solution(mesh):
    return jax.shard_map(
        local,
        mesh=mesh,
        in_specs=(
            P("grp", "sub", None, None),
            P("grp", "sub"),
            P("grp", "sub", None, None),
            P("grp", "sub", None, None),
            P("grp", "sub", None, None),
            P("grp", "sub", None),
            P("sub", "grp", None),
        ),
        out_specs=(P("grp", "sub", None, None), P("grp", "sub", None, None)),
        check_vma=False,
    )
```

profile of v0, /device:TPU:1, one launch (start us, length us, event | category | flops | bytes accessed | tf_op | source)
XLA Modules:
  0.0 832.8 jit_solution(642383770802080915)
XLA Ops:
  7.2 0.9 fusion.82
  8.1 1.3 broadcast_multiply_fusion.1
  9.4 4.0 collective-permute-start
  13.5 4.9 collective-permute-done
  18.5 1.8 fusion.42
  20.3 1.3 collective-permute-start.1
  21.7 7.8 collective-permute-done.1
  29.7 3.2 collective-permute-start.2
  33.1 3.2 collective-permute-done.2
  36.4 1.9 fusion.29
  38.3 3.7 convolution_bitcast_fusion.2
  42.0 38.6 %reduce-scatter.4.cloned.1.call-done = f32[256,256]{1,0:T(8,128)} async-done(((f32[2048,256]{1,0:T(8,128)}), f32[256,256]{1,0:T(8,128)}) %reduce-scatter.4.cloned.1.call-update) | async-done | bytes 262160 | tf_op jit(solution)/shard_map/reduce_scatter | solution.py:74
  80.6 4.9 convolution_bitcast_fusion.5
  85.8 65.4 %all-reduce.5.cloned.1.call-done = f32[2048,256]{0,1:T(8,128)} async-done(((f32[2048,256]{0,1:T(8,128)}), f32[2048,256]{0,1:T(8,128)}) %all-reduce.5.cloned.1.call-update) | async-done | bytes 2097168 | tf_op jit(solution)/shard_map/psum | solution.py:81
  151.2 3.1 fusion.45
  154.3 1.8 fusion.78
  156.2 1.8 add_bitcast_fusion.2
  158.1 1.6 collective-permute-start.3
  159.7 5.7 collective-permute-done.3
  166.2 70.6 %all-reduce = (f32[256]{0:T(256)S(1)}, f32[256]{0:T(256)S(1)}) all-reduce(f32[256]{0:T(256)S(1)} %get-tuple-element.3, f32[256]{0:T(256)S(1)} %get-tuple-element.2), channel_id=1, replica_groups=mesh['sub'=16,'grp'=8] {'sub','grp'}, use_global_device_ids=true, to_apply=%region_1.0 | all-reduce | flops 512 | bytes 4096 | tf_op jit(solution)/shard_map/psum | solution.py:46
  236.8 2.1 multiply_subtract_fusion.2
  238.9 2.5 collective-permute-start.4
  241.4 4.6 collective-permute-done.4
  246.1 1.8 fusion.39
  248.0 1.3 collective-permute-start.5
  249.4 7.5 collective-permute-done.5
  258.0 67.7 %psum.66 = f32[256]{0:T(256)S(1)} all-reduce(f32[256]{0:T(256)S(1)} %multiply_reduce_fusion.3), channel_id=1, replica_groups=mesh['sub'=16,'grp'=8] {'sub','grp'}, use_global_device_ids=true, to_apply=%region_7.0 | all-reduce | flops 256 | bytes 2048 | tf_op jit(solution)/shard_map/psum | solution.py:46
  325.7 2.1 multiply_add_fusion.2
  327.8 2.6 collective-permute-start.6
  330.5 4.6 collective-permute-done.6
  335.1 1.0 copy-done.20
  336.1 1.9 fusion.28
  338.0 3.7 convolution_bitcast_fusion.1
  341.7 32.0 %reduce-scatter.6.cloned.1.call-done = f32[256,256]{1,0:T(8,128)} async-done(((f32[2048,256]{1,0:T(8,128)}), f32[256,256]{1,0:T(8,128)}) %reduce-scatter.6.cloned.1.call-update) | async-done | bytes 262160 | tf_op jit(solution)/shard_map/reduce_scatter | solution.py:74
  373.7 4.9 convolution_bitcast_fusion.4
  378.7 65.6 %all-reduce.7.cloned.1.call-done = f32[2048,256]{0,1:T(8,128)} async-done(((f32[2048,256]{0,1:T(8,128)}), f32[2048,256]{0,1:T(8,128)}) %all-reduce.7.cloned.1.call-update) | async-done | bytes 2097168 | tf_op jit(solution)/shard_map/psum | solution.py:81
  444.4 3.1 fusion.48
  447.5 1.8 fusion.75
  449.3 1.8 add_bitcast_fusion.1
  451.2 1.3 collective-permute-start.7
  452.6 5.7 collective-permute-done.7
  459.4 71.1 %psum.68 = f32[256]{0:T(256)S(1)} all-reduce(f32[256]{0:T(256)S(1)} %multiply_reduce_fusion.2), channel_id=1, replica_groups=mesh['sub'=16,'grp'=8] {'sub','grp'}, use_global_device_ids=true, to_apply=%region_11.0 | all-reduce | flops 256 | bytes 2048 | tf_op jit(solution)/shard_map/psum | solution.py:88
  530.5 2.1 multiply_subtract_fusion.1
  532.6 2.5 collective-permute-start.8
  535.1 4.6 collective-permute-done.8
  539.8 1.8 fusion.36
  541.6 1.3 collective-permute-start.9
  543.0 7.5 collective-permute-done.9
  551.6 67.7 %psum.69 = f32[256]{0:T(256)S(1)} all-reduce(f32[256]{0:T(256)S(1)} %multiply_reduce_fusion.1), channel_id=1, replica_groups=mesh['sub'=16,'grp'=8] {'sub','grp'}, use_global_device_ids=true, to_apply=%region_13.0 | all-reduce | flops 256 | bytes 2048 | tf_op jit(solution)/shard_map/psum | solution.py:46
  619.3 1.8 multiply_add_fusion.1
  621.1 2.4 collective-permute-start.10
  623.6 4.8 collective-permute-done.10
  628.4 1.9 fusion.27
  630.3 3.7 convolution_bitcast_fusion
  634.3 31.8 %reduce-scatter.8.cloned.1.call-done = f32[256,256]{1,0:T(8,128)} async-done(((f32[2048,256]{1,0:T(8,128)}), f32[256,256]{1,0:T(8,128)}) %reduce-scatter.8.cloned.1.call-update) | async-done | bytes 262160 | tf_op jit(solution)/shard_map/reduce_scatter | solution.py:74
  666.1 4.9 convolution_bitcast_fusion.3
  671.0 65.7 %all-reduce.9.cloned.1.call-done = f32[2048,256]{0,1:T(8,128)} async-done(((f32[2048,256]{0,1:T(8,128)}), f32[2048,256]{0,1:T(8,128)}) %all-reduce.9.cloned.1.call-update) | async-done | bytes 2097168 | tf_op jit(solution)/shard_map/psum | solution.py:81
  736.7 3.1 fusion.51
  739.8 1.8 fusion.72
  741.7 1.8 add_bitcast_fusion
  743.6 1.3 collective-permute-start.11
  744.9 5.7 collective-permute-done.11
  750.9 70.7 %psum.71 = f32[256]{0:T(256)S(1)} all-reduce(f32[256]{0:T(256)S(1)} %multiply_reduce_fusion), channel_id=1, replica_groups=mesh['sub'=16,'grp'=8] {'sub','grp'}, use_global_device_ids=true, to_apply=%region_17.0 | all-reduce | flops 256 | bytes 2048 | tf_op jit(solution)/shard_map/psum | solution.py:88
  821.6 4.1 multiply_subtract_fusion
  (121 shorter events, 6.5 us)
Async XLA Ops:
  7.2 11.3 %copy-start = (bf16[1,4,512,512]{3,2,1,0:T(8,128)(2,1)S(1)}, bf16[1,4,512,512]{3,2,1,0:T(8,128)(2,1)}, u32[]{:S(2)}) copy-start(bf16[1,4,512,512]{3,2,1,0:T(8,128)(2,1)} %param.10) | copy-start | bytes 6291460
  7.2 73.4 %reduce-scatter.4.cloned.1.call-start = ((), (), s32[]{:S(2)}) async-start(), calls=%async_computation.3 | async-start | bytes 2359296 | tf_op jit(solution)/shard_map/reduce_scatter | solution.py:74
  9.4 8.9 %collective-permute-start = (f32[1,1,256,256]{3,2,1,0:T(8,128)S(1)}, f32[1,1,256,256]{3,2,1,0:T(8,128)S(1)}, u32[]{:S(2)}, u32[]{:S(2)}) collective-permute-start(f32[1,1,256,256]{3,2,1,0:T(8,128)S(1)} %slice.120), channel_id=1, source_target_pairs={{0,8},{8,16},{16,24},{24,32},{32,40},{40,48},{48,56},{56,64},{64,7... | collective-permute-start | bytes 786440 | tf_op jit(solution)/shard_map/ppermute | solution.py:15
  20.3 9.2 %collective-permute-start.1 = (f32[1,1,256,256]{3,2,1,0:T(8,128)S(1)}, f32[1,1,256,256]{3,2,1,0:T(8,128)S(1)}, u32[]{:S(2)}, u32[]{:S(2)}) collective-permute-start(f32[1,1,256,256]{3,2,1,0:T(8,128)S(1)} %slice.124), channel_id=1, source_target_pairs={{8,0},{16,8},{24,16},{32,24},{40,32},{48,40},{56,48},{64,56},{72,6... | collective-permute-start | bytes 786440 | tf_op jit(solution)/shard_map/ppermute | solution.py:15
  29.7 6.7 copy-start.9
  29.7 135.8 %copy-start.8 = (f32[1,4,256,256]{3,2,1,0:T(8,128)}, f32[1,4,256,256]{3,2,1,0:T(8,128)S(1)}, u32[]{:S(2)}) copy-start(f32[1,4,256,256]{3,2,1,0:T(8,128)S(1)} %get-tuple-element.9) | copy-start | bytes 3145732
  29.7 6.6 copy-start.17
  29.7 6.5 collective-permute-start.2
  33.0 5.2 copy-start.33
  36.4 1.9 copy-start.18
  42.0 109.2 %all-reduce.5.cloned.1.call-start = ((), (), s32[]{:S(2)}) async-start(), calls=%async_computation.4 | async-start | bytes 4194304 | tf_op jit(solution)/shard_map/psum | solution.py:81
  85.5 288.2 %reduce-scatter.6.cloned.1.call-start = ((), (), s32[]{:S(2)}) async-start(), calls=%async_computation.5 | async-start | bytes 2359296 | tf_op jit(solution)/shard_map/reduce_scatter | solution.py:74
  151.2 5.0 copy-start.5
  151.2 5.0 copy-start.10
  151.2 5.0 copy-start.19
  158.0 7.9 copy-start.14
  158.0 7.4 copy-start.16
  158.1 7.4 collective-permute-start.3
  159.7 6.3 copy-start.25
  165.5 0.7 copy-start.29
  238.9 18.0 %copy-start.4 = (f32[1,4,256,256]{3,2,1,0:T(8,128)}, f32[1,4,256,256]{3,2,1,0:T(8,128)S(1)}, u32[]{:S(2)}) copy-start(f32[1,4,256,256]{3,2,1,0:T(8,128)S(1)} %multiply_subtract_fusion.2) | copy-start | bytes 3145732
  238.9 7.1 collective-permute-start.4
  248.0 8.9 %copy-start.11 = (f32[1,4,256,512]{3,2,1,0:T(8,128)}, f32[1,4,256,512]{3,2,1,0:T(8,128)S(1)}, u32[]{:S(2)}) copy-start(f32[1,4,256,512]{3,2,1,0:T(8,128)S(1)} %fusion.39) | copy-start | bytes 6291460
  248.0 8.9 %collective-permute-start.5 = (f32[1,1,256,256]{3,2,1,0:T(8,128)S(1)}, f32[1,1,256,256]{3,2,1,0:T(8,128)S(1)}, u32[]{:S(2)}, u32[]{:S(2)}) collective-permute-start(f32[1,1,256,256]{3,2,1,0:T(8,128)S(1)} %slice.134), channel_id=1, source_target_pairs={{8,0},{16,8},{24,16},{32,24},{40,32},{48,40},{56,48},{64,56},{72,6... | collective-permute-start | bytes 786440 | tf_op jit(solution)/shard_map/ppermute | solution.py:15
  249.4 7.5 copy-start.27
  256.9 0.7 copy-start.31
  327.8 7.2 collective-permute-start.6
  335.1 1.0 copy-start.20
  341.7 102.7 %all-reduce.7.cloned.1.call-start = ((), (), s32[]{:S(2)}) async-start(), calls=%async_computation.6 | async-start | bytes 4194304 | tf_op jit(solution)/shard_map/psum | solution.py:81
  378.7 287.4 %reduce-scatter.8.cloned.1.call-start = ((), (), s32[]{:S(2)}) async-start(), calls=%async_computation.7 | async-start | bytes 2359296 | tf_op jit(solution)/shard_map/reduce_scatter | solution.py:74
  444.4 5.0 copy-start.6
  444.4 5.0 copy-start.21
  451.2 7.2 copy-start.15
  451.2 7.1 collective-permute-start.7
  452.6 5.7 copy-start.26
  458.3 0.7 copy-start.30
  532.5 18.0 %copy-start.3 = (f32[1,4,256,256]{3,2,1,0:T(8,128)}, f32[1,4,256,256]{3,2,1,0:T(8,128)S(1)}, u32[]{:S(2)}) copy-start(f32[1,4,256,256]{3,2,1,0:T(8,128)S(1)} %multiply_subtract_fusion.1) | copy-start | bytes 3145732
  532.6 7.1 collective-permute-start.8
  541.6 8.9 %copy-start.12 = (f32[1,4,256,512]{3,2,1,0:T(8,128)}, f32[1,4,256,512]{3,2,1,0:T(8,128)S(1)}, u32[]{:S(2)}) copy-start(f32[1,4,256,512]{3,2,1,0:T(8,128)S(1)} %fusion.36) | copy-start | bytes 6291460
  541.6 8.9 %collective-permute-start.9 = (f32[1,1,256,256]{3,2,1,0:T(8,128)S(1)}, f32[1,1,256,256]{3,2,1,0:T(8,128)S(1)}, u32[]{:S(2)}, u32[]{:S(2)}) collective-permute-start(f32[1,1,256,256]{3,2,1,0:T(8,128)S(1)} %slice.144), channel_id=1, source_target_pairs={{8,0},{16,8},{24,16},{32,24},{40,32},{48,40},{56,48},{64,56},{72,6... | collective-permute-start | bytes 786440 | tf_op jit(solution)/shard_map/ppermute | solution.py:15
  543.0 7.5 copy-start.28
  550.5 0.7 copy-start.32
  621.1 7.4 copy-start.1
  621.1 7.2 collective-permute-start.10
  628.4 1.9 copy-start.22
  634.1 102.6 %all-reduce.9.cloned.1.call-start = ((), (), s32[]{:S(2)}) async-start(), calls=%async_computation.8 | async-start | bytes 4194304 | tf_op jit(solution)/shard_map/psum | solution.py:81
  736.7 5.0 copy-start.2
  736.7 5.0 copy-start.7
  736.7 5.0 copy-start.23
  743.5 7.2 copy-start.13
  743.6 7.1 collective-permute-start.11
  744.9 5.7 copy-start.24
Sparse Core Ops, SparseCore 0:
  42.1 38.4 reduce-scatter.3
  85.7 65.4 all-reduce.4
  341.8 31.8 reduce-scatter.5
  378.8 65.5 all-reduce.6
  634.2 31.8 reduce-scatter.7
  671.1 65.4 all-reduce.8
where the time goes:
time: 841 us; the launch traced here: 833 us
  waiting for transfers between devices  366 us (44%)
  blocking collectives  348 us (41%)
  matrix products  57.2 us (7%)
  starting transfers between devices  25.7 us (3%)
  other arithmetic  16.7 us (2%)
  between operations  15.2 us (2%)
    psum x3, blocking collectives, residual_sum(): return lax.psum(inner(resid, precond), ('sub', 'grp'))  206 us
    psum x3, waiting for transfers between devices, local(): solved = lax.psum(partial_solved, 'grp')  197 us
    psum x2, blocking collectives, local(): alpha = rz_now / lax.psum(inner(direction, image), ('sub', 'grp'))  142 us
    reduce_scatter x3, waiting for transfers between devices, local(): lax.psum_scatter(jnp.einsum('skn,srk->nr', corner_onehot, corner_vals, pr...  102 us
    ppermute x12, waiting for transfers between devices, passed_along(): return lax.ppermute(block, axis, route)  66.6 us
    ppermute x12, starting transfers between devices, passed_along(): return lax.ppermute(block, axis, route)  25.1 us
  transfers between devices with their start and end apart: 18, of which 18 were waited for; matrix products, arithmetic and copies ran while one was open for 0% of the time, Pallas kernels for 0%

commit v1 on v0

v1 whole, which is shorter than its diff:
```python
import jax
import jax.numpy as jnp
from jax import lax
from jax.experimental import pallas as pl
from jax.experimental.pallas import tpu as pltpu
from jax.sharding import PartitionSpec as P

MESH = pl.DeviceIdType.MESH
F32, BF16, I32 = jnp.float32, jnp.bfloat16, jnp.int32
NSUB, NGRP, NY = 16, 8, 4
SUBS, H, PS, NC, NCO = 4, 256, 512, 32, 2048
LANES, CHUNKS, PAIRS = 128, 2, 5
OWN = SUBS * NC
LEFT, RIGHT = 0, 1


def remote(src, dst, send_sem, recv_sem, device):
    return pltpu.make_async_remote_copy(
        src_ref=src,
        dst_ref=dst,
        send_sem=send_sem,
        recv_sem=recv_sem,
        device_id=device,
        device_id_type=MESH,
    )


def split(value):
    high = value.astype(BF16)
    low = (value - high.astype(F32)).astype(BF16)
    return high, low


def colsum(value):
    return jnp.sum(value, axis=0, keepdims=True)


def chunks(body):
    def step(k, carry):
        body(k)
        return carry

    lax.fori_loop(0, CHUNKS, step, 0)


def block(i):
    return pl.ds(H * i, H)


def kernel(
    rhs_h, counts_s, solve_h, dirichlet_h, coupling_h, map_h, coarse_h, x_h, res_h,
    rhs_v, sc, dm, cext, ci, cis, cmt, cnt, onehot, rowhot, a_part, a_split, g_part, ring_a, ring_b,
    gs, ext, mask, r, u, w, m0, n0, m1, p, s, x, vs, wb, from_left, from_right, corners, cown, bext, red_a, red_b,
    load_sem, cm_send, cm_recv, misc_send, misc_recv, halo_send, halo_recv, ex_send, ex_recv,
    bk_send, bk_recv, ag_send, ag_recv, ra_send, ra_recv, rb_send, rb_recv, ring_send, ring_recv,
):
    sub, grp = lax.axis_index("sub"), lax.axis_index("grp")
    right, left = lax.rem(sub + 1, NSUB), lax.rem(sub + NSUB - 1, NSUB)
    y, core = lax.div(grp, 2), lax.rem(grp, 2)
    mate = 2 * y + 1 - core
    to_right, to_left, to_mate = {"sub": right}, {"sub": left}, {"grp": mate}

    def grp_at(step):
        return 2 * lax.rem(y + step, NY) + core

    loads = [
        pltpu.make_async_copy(map_h, cmt.at[grp], load_sem.at[0]),
        pltpu.make_async_copy(coupling_h.at[0], cext.at[pl.ds(1, SUBS)], load_sem.at[1]),
        pltpu.make_async_copy(rhs_h.at[0], rhs_v, load_sem.at[2]),
        pltpu.make_async_copy(coarse_h.at[0], ci, load_sem.at[3]),
        pltpu.make_async_copy(dirichlet_h.at[0], dm, load_sem.at[4]),
        pltpu.make_async_copy(solve_h.at[0], sc.at[:, pl.ds(0, PS)], load_sem.at[5]),
    ]
    for load in loads:
        load.start()

    barrier = pltpu.get_barrier_semaphore()
    for i in range(1, NGRP):
        pl.semaphore_signal(barrier, inc=1, device_id={"grp": lax.rem(grp + i, NGRP)}, device_id_type=MESH)
    for i in range(1, NSUB):
        pl.semaphore_signal(barrier, inc=1, device_id={"sub": lax.rem(sub + i, NSUB)}, device_id_type=MESH)
    pl.semaphore_wait(barrier, NGRP + NSUB - 2)

    def map_copy(i):
        peer = lax.rem(grp + i, NGRP)
        return remote(cmt.at[grp], cmt.at[grp], cm_send.at[i], cm_recv.at[i], {"grp": peer})

    def map_arrival(i):
        slot = lax.rem(grp + NGRP - i, NGRP)
        return remote(cmt.at[slot], cmt.at[slot], cm_send.at[i], cm_recv.at[i], to_mate)

    count_copy = remote(cnt.at[0], cnt.at[1], misc_send.at[0], misc_recv.at[0], to_right)
    cpl_right = remote(
        cext.at[SUBS, :, pl.ds(H, H)], cext.at[0, :, pl.ds(H, H)], misc_send.at[1], misc_recv.at[1], to_right
    )
    cpl_left = remote(
        cext.at[1, :, pl.ds(0, H)], cext.at[SUBS + 1, :, pl.ds(0, H)], misc_send.at[2], misc_recv.at[2], to_left
    )
    mate_copy = remote(a_part.at[core], a_part.at[core], misc_send.at[3], misc_recv.at[3], to_mate)
    mate_arrival = remote(a_part.at[1 - core], a_part.at[1 - core], misc_send.at[3], misc_recv.at[3], to_mate)
    up, down, far = lax.rem(y + 1, NY), lax.rem(y + 3, NY), lax.rem(y + 2, NY)
    to_up, to_down = {"grp": 2 * up + core}, {"grp": 2 * down + core}
    ring_copies = [
        remote(g_part.at[far, pl.ds(0, 2)], ring_a.at[0], ring_send.at[0], ring_recv.at[0], to_up),
        remote(g_part.at[far, pl.ds(2, 2)], ring_a.at[1], ring_send.at[1], ring_recv.at[1], to_down),
        remote(g_part.at[up], ring_b.at[0], ring_send.at[2], ring_recv.at[2], to_up),
        remote(g_part.at[down], ring_b.at[1], ring_send.at[3], ring_recv.at[3], to_down),
    ]

    def halo_copy(k):
        return remote(
            r.at[k, block(SUBS)], r.at[k, block(0)], halo_send.at[k], halo_recv.at[k], to_right
        )

    def face_left(op, k):
        return remote(
            wb.at[op % 2, k, 0, pl.ds(0, H)], from_right.at[op, k],
            ex_send.at[op, LEFT, k], ex_recv.at[op, LEFT, k], to_left,
        )

    def face_right(op, k):
        return remote(
            wb.at[op % 2, k, SUBS - 1, pl.ds(H, H)], from_left.at[op, k],
            ex_send.at[op, RIGHT, k], ex_recv.at[op, RIGHT, k], to_right,
        )

    def back_left(f, k):
        return remote(
            bext.at[f, k, pl.ds(NC, NC)], bext.at[f, k, pl.ds(NC + OWN, NC)],
            bk_send.at[f, LEFT, k], bk_recv.at[f, LEFT, k], to_left,
        )

    def back_right(f, k):
        return remote(
            bext.at[f, k, pl.ds(OWN, NC)], bext.at[f, k, pl.ds(0, NC)],
            bk_send.at[f, RIGHT, k], bk_recv.at[f, RIGHT, k], to_right,
        )

    def corner_copy(f, k, i):
        device = to_mate if i == 0 else {"grp": grp_at(i)}
        mine = corners.at[f, k, grp]
        return remote(mine, mine, ag_send.at[f, k, i], ag_recv.at[f, k, i], device)

    def corner_arrival(f, k, i):
        slot = mate if i == 0 else grp_at(NY - i)
        there = corners.at[f, k, slot]
        return remote(there, there, ag_send.at[f, k, i], ag_recv.at[f, k, i], to_mate)

    def corner_forward(f, k, i):
        there = corners.at[f, k, grp_at(NY - i)]
        return remote(there, there, ag_send.at[f, k, NY - 1 + i], ag_recv.at[f, k, NY - 1 + i], to_mate)

    def corner_forwarded(f, k, i):
        there = corners.at[f, k, 2 * lax.rem(y + NY - i, NY) + 1 - core]
        return remote(there, there, ag_send.at[f, k, NY - 1 + i], ag_recv.at[f, k, NY - 1 + i], to_mate)

    def sum_a(t, i):
        mine = red_a.at[t, grp]
        return remote(mine, mine, ra_send.at[t, i], ra_recv.at[t, i], {"grp": lax.rem(grp + i, NGRP)})

    def sum_a_arrival(t, i):
        there = red_a.at[t, lax.rem(grp + NGRP - i, NGRP)]
        return remote(there, there, ra_send.at[t, i], ra_recv.at[t, i], to_mate)

    def sum_b(t, i):
        mine = red_b.at[t, sub]
        return remote(mine, mine, rb_send.at[t, i], rb_recv.at[t, i], {"sub": lax.rem(sub + i, NSUB)})

    def sum_b_arrival(t, i):
        there = red_b.at[t, lax.rem(sub + NSUB - i, NSUB)]
        return remote(there, there, rb_send.at[t, i], rb_recv.at[t, i], to_right)


    def split_vector(vector, k):
        for i in range(PAIRS):
            high, low = split(vector[k, block(i)])
            vs[k, block(i), pl.ds(0, LANES)] = high
            vs[k, block(i), pl.ds(LANES, LANES)] = low

    def apply_panel(op, k, j, solve):
        faces = vs[k, pl.ds(pl.multiple_of(H * j, H), PS), :]
        both = jnp.dot((sc if solve else dm)[j], faces, preferred_element_type=F32)
        both = both[:, :LANES] + both[:, LANES:]
        wb[op % 2, k, j] = both[:PS]
        if solve:
            f = op // 2
            values = both[PS : PS + NC] + both[PS + NC :]
            rows = pl.ds(pl.multiple_of(NC * j, NC), NC)
            cown[f, k, rows] = values

    def start(op, k, vector, last=False):
        solve = op % 2 == 1
        if op >= 2:
            face_left(op - 2, k).wait_send()
            face_right(op - 2, k).wait_send()
        split_vector(vector, k)

        def outer(t, carry):
            apply_panel(op, k, (SUBS - 1) * t, solve)
            return carry

        lax.fori_loop(0, 2, outer, 0)
        face_left(op, k).start()
        if not last:
            face_right(op, k).start()

        def inner(t, carry):
            apply_panel(op, k, 1 + t, solve)
            return carry

        lax.fori_loop(0, 2, inner, 0)
        if solve:
            f = op // 2
            corners[f, k, grp] = cown[f, k]
            for i in range(NY):
                corner_copy(f, k, i).start()

    def gather(f, k):
        for i in range(1, NY):
            corner_arrival(f, k, i).wait_recv()
            corner_forward(f, k, i).start()

    def coarse(f, k, last=False):
        corner_arrival(f, k, 0).wait_recv()
        for i in range(1, NY):
            corner_forwarded(f, k, i).wait_recv()
        high, low = split(corners[f, k].reshape(NGRP * OWN, LANES))
        both = jnp.dot(gs[...], jnp.concatenate([high, low], axis=1), preferred_element_type=F32)
        both = both[:, :LANES] + both[:, LANES:]
        bext[f, k, pl.ds(NC, OWN)] = both[:OWN] + both[OWN:]
        back_left(f, k).start()
        if not last:
            back_right(f, k).start()

    def image(op, k, i, scale=None):
        before = from_left[op, k] if i == 0 else wb[op % 2, k, i - 1, pl.ds(H, H)]
        after = from_right[op, k] if i == SUBS else wb[op % 2, k, i, pl.ds(0, H)]
        value = before + after
        if op % 2 == 1:
            high, low = split(bext[op // 2, k, pl.ds(NC * i, 2 * NC)])
            faces = jnp.concatenate([high, low, high, low], axis=0)
            value = value + jnp.dot(ext[i], faces, preferred_element_type=F32)
        else:
            value = 0.25 * value
        return jnp.where(mask[i] > 0.0, value, 0.0)

    def arrive(op, k, last=False):
        face_left(op, k).wait_recv()
        if op % 2 == 1:
            back_left(op // 2, k).wait_recv()
        if not last:
            face_right(op, k).wait_recv()
            if op % 2 == 1:
                back_right(op // 2, k).wait_recv()

    def finish(op, k, out):
        arrive(op, k)
        for i in range(PAIRS):
            out[k, block(i)] = image(op, k, i)

    def product(first, second, k):
        return colsum(first[k, pl.ds(H, SUBS * H)] * second[k, pl.ds(H, SUBS * H)])

    def put_sums(t, k, values):
        for i, value in enumerate(values):
            red_a[t, grp, k, pl.ds(i, 1)] = value

    def send_sums(t):
        for i in range(1, NGRP):
            sum_a(t, i).start()

    def pass_sums(t):
        for i in range(1, NGRP):
            sum_a_arrival(t, i).wait_recv()
        red_b[t, sub] = jnp.sum(red_a[t], axis=0)
        for i in range(1, NSUB):
            sum_b(t, i).start()

    def get_sums(t):
        for i in range(1, NSUB):
            sum_b_arrival(t, i).wait_recv()

    def sums(t, k):
        total = jnp.sum(red_b[t, :, k], axis=0)
        return [total[i : i + 1] for i in range(3)]

    load = loads[0]
    load.wait()
    for i in range(1, NGRP):
        map_copy(i).start()
    rows = lax.broadcasted_iota(I32, (H, LANES), 0)
    for c in range(SUBS):
        live = counts_s[0, c]
        if c == SUBS - 1:
            live = jnp.where(sub == NSUB - 1, 0, live)
            cnt[0] = jnp.full((8, LANES), live, I32)
        mask[c + 1] = (rows < live).astype(F32)
    count_copy.start()
    loads[1].wait()
    cpl_right.start()
    cpl_left.start()
    loads[2].wait()
    for c in (3, 0, 1, 2):
        turned = rhs_v[c].T
        for k in range(CHUNKS):
            r[k, block(c + 1)] = jnp.where(
                mask[c + 1] > 0.0, turned[:, LANES * k : LANES * (k + 1)], 0.0
            )
        if c == SUBS - 1:
            for k in range(CHUNKS):
                halo_copy(k).start()

    loads[3].wait()
    for i in range(4):
        high, low = split(ci[pl.ds(64 * i, 64)])
        cis[pl.ds(64 * i, 64)] = high
        cis[pl.ds(256 + 64 * i, 64)] = low
    for i in range(1, NGRP):
        map_arrival(i).wait_recv()

    def columns(q, carry):
        for c in range(2):
            wanted = cmt[2 * q + c, pl.ds(0, 1)]

            def fill(t, inner):
                first = pl.multiple_of(256 * t, 256)
                at = lax.broadcasted_iota(I32, (256, LANES), 0) + first
                onehot[pl.ds(first, 256), pl.ds(LANES * c, LANES)] = (at == wanted).astype(F32).astype(BF16)
                return inner

            lax.fori_loop(0, NCO // 256, fill, 0)
        both = jnp.dot(cis[...], onehot[...], preferred_element_type=F32)
        a_part[core, q] = both[:256] + both[256:]
        return carry

    lax.fori_loop(0, NY, columns, 0)
    mate_copy.start()

    loads[4].wait()
    for j in range(SUBS):
        for a, b in ((0, 1), (1, 0)):
            dm[j, block(a), block(b)] = -dm[j, block(a), block(b)]
    count_copy.wait_recv()
    mask[0] = (rows < cnt[1, pl.ds(0, 1)]).astype(F32)

    def first(k):
        halo_copy(k).wait_recv()
        start(0, k, r)

    chunks(first)

    loads[5].wait()
    cpl_right.wait_recv()
    cpl_left.wait_recv()
    for j in range(SUBS):
        for a, b in ((0, 1), (1, 0)):
            sc[j, block(a), block(b)] = -sc[j, block(a), block(b)]
        for half in range(2):
            part = cext[j + 1, :, block(half)]
            high, low = split(part if half else -part)
            sc[j, pl.ds(PS, NC), block(half)] = high
            sc[j, pl.ds(PS + NC, NC), block(half)] = low
    for i in range(PAIRS):
        both = jnp.concatenate([cext[i, :, block(1)], -cext[i + 1, :, block(0)]], axis=0)
        high = both.astype(BF16).astype(F32)
        low = both - high
        ext[i] = jnp.concatenate([high, high, low, low], axis=0).T.astype(BF16)

    mate_arrival.wait_recv()
    for q in range(NY):
        for c in range(2):
            high, low = split(a_part[c, q])
            a_split[q, block(c), pl.ds(0, 256)] = high
            a_split[q, block(c), pl.ds(256, 256)] = low
    lane = lax.broadcasted_iota(I32, (LANES, LANES), 1).astype(F32)
    base = (2 * NGRP * 32 * y).astype(F32)
    for q in range(NY):
        wanted = jnp.broadcast_to(cmt[2 * q + core, pl.ds(0, 1)], (LANES, LANES)).astype(F32).T
        for t in range(4):
            rowhot[pl.ds(LANES * q, LANES), pl.ds(LANES * t, LANES)] = (
                wanted == lane + (base + 128.0 * t)
            ).astype(F32).astype(BF16)

    def rows_of(q, carry):
        both = jnp.dot(rowhot[...], a_split[q], preferred_element_type=F32)
        both = both[:, :256] + both[:, 256:]
        for chip in range(NY):
            g_part[chip, q] = both[LANES * chip : LANES * (chip + 1)]
        return carry

    lax.fori_loop(0, NY, rows_of, 0)
    ring_copies[0].start()
    ring_copies[1].start()

    def second(k):
        finish(0, k, u)
        start(1, k, u)

    chunks(second)

    ring_copies[0].wait_recv()
    g_part[up, pl.ds(0, 2)] = g_part[up, pl.ds(0, 2)] + ring_a[0]
    ring_copies[2].start()
    ring_copies[1].wait_recv()
    g_part[down, pl.ds(2, 2)] = g_part[down, pl.ds(2, 2)] + ring_a[1]
    ring_copies[3].start()
    chunks(lambda k: gather(0, k))
    ring_copies[2].wait_recv()
    ring_copies[3].wait_recv()
    for q in range(NY):
        high, low = split(g_part[y, q] + ring_b[0, q] + ring_b[1, q])
        gs[pl.ds(0, OWN), pl.ds(256 * q, 256)] = high
        gs[pl.ds(OWN, OWN), pl.ds(256 * q, 256)] = low

    chunks(lambda k: coarse(0, k))

    def third(k):
        finish(1, k, w)
        put_sums(0, k, [product(r, u, k), product(u, w, k), jnp.zeros((1, LANES), F32)])
        start(2, k, w)

    chunks(third)
    send_sums(0)

    def fourth(k):
        finish(2, k, m0)
        start(3, k, m0)

    chunks(fourth)
    pass_sums(0)
    chunks(lambda k: gather(1, k))
    chunks(lambda k: coarse(1, k))
    get_sums(0)

    def scalars(k):
        rz0, den0, _ = sums(0, k)
        return rz0, den0, rz0 / den0

    def fifth(k):
        _, _, alpha = scalars(k)
        halo_copy(k).wait_send()
        arrive(3, k)
        for i in range(PAIRS):
            here = (k, block(i))
            n0[here] = image(3, k, i)
            p[here] = u[here]
            s[here] = w[here]
            x[here] = alpha * u[here]
            r[here] = r[here] - alpha * w[here]
            u[here] = u[here] - alpha * m0[here]
            w[here] = w[here] - alpha * n0[here]
        put_sums(1, k, [product(r, u, k), product(u, w, k), product(u, s, k)])
        start(4, k, w)

    chunks(fifth)
    send_sums(1)

    def sixth(k):
        finish(4, k, m1)
        start(5, k, m1, last=True)

    chunks(sixth)
    pass_sums(1)
    chunks(lambda k: gather(2, k))
    get_sums(1)

    def scalars_one(k):
        rz0, den0, alpha0 = scalars(k)
        rz1, uw, us = sums(1, k)
        beta = rz1 / rz0
        den1 = uw + beta * (us + us) + beta * beta * den0
        return alpha0, rz1, den1, beta, rz1 / den1

    def seventh(k):
        alpha0, _, _, beta, alpha = scalars_one(k)
        for i in range(PAIRS):
            here = (k, block(i))
            p[here] = u[here] + beta * p[here]
            s[here] = w[here] + beta * s[here]
            x[here] = x[here] + alpha * p[here]
            r[here] = r[here] - alpha * s[here]
            u[here] = u[here] - alpha * (m1[here] + beta * m0[here])
            w[here] = w[here] - (alpha * beta) * n0[here]
        coarse(2, k, last=True)
        corner = cown[0, k] - alpha0 * cown[1, k] - alpha * (cown[2, k] + beta * cown[1, k])
        local = colsum(corner * bext[2, k, pl.ds(NC, OWN)])
        for j in range(SUBS):
            local = local + colsum(u[k, pl.ds(H * j, PS)] * wb[1, k, j])
        put_sums(2, k, [product(r, u, k), product(u, w, k) - alpha * local, product(u, s, k)])

    chunks(seventh)
    send_sums(2)
    pass_sums(2)
    chunks(lambda k: arrive(5, k, last=True))
    get_sums(2)

    stores = []
    for c in range(SUBS):
        sides_x, sides_r = [], []
        for k in range(CHUNKS):
            _, rz1, den1, _, alpha1 = scalars_one(k)
            rz2, uw, us = sums(2, k)
            beta = rz2 / rz1
            den2 = uw + beta * (us + us) + beta * beta * den1
            alpha = rz2 / den2
            here = (k, block(c + 1))
            end = w[here] - alpha1 * image(5, k, c + 1)
            sides_x.append(x[here] + alpha * (u[here] + beta * p[here]))
            sides_r.append(r[here] - alpha * (end + beta * s[here]))
        rhs_v[c] = jnp.concatenate(sides_x, axis=1).T
        ci[:, pl.ds(H * c, H)] = jnp.concatenate(sides_r, axis=1).T
        stores.append(pltpu.make_async_copy(rhs_v.at[c], x_h.at[0, c], load_sem.at[6 + 2 * c]))
        stores.append(
            pltpu.make_async_copy(ci.at[:, pl.ds(H * c, H)], res_h.at[0, c], load_sem.at[7 + 2 * c])
        )
        stores[-2].start()
        stores[-1].start()

    for i in range(1, NGRP):
        map_copy(i).wait_send()
    for copy in (count_copy, cpl_right, cpl_left, mate_copy, *ring_copies):
        copy.wait_send()

    def drain(k):
        face_left(4, k).wait_send()
        face_right(4, k).wait_send()
        face_left(5, k).wait_send()
        for f in range(3):
            back_left(f, k).wait_send()
            if f < 2:
                back_right(f, k).wait_send()
            for i in range(NY):
                corner_copy(f, k, i).wait_send()
            for i in range(1, NY):
                corner_forward(f, k, i).wait_send()

    chunks(drain)
    for t in range(3):
        for i in range(1, NGRP):
            sum_a(t, i).wait_send()
        for i in range(1, NSUB):
            sum_b(t, i).wait_send()
    for copy in stores:
        copy.wait()


def local(rhs, counts, solve_panel, dirichlet_panel, coupling, corner_map, coarse_inverse):
    vector = pltpu.VMEM((CHUNKS, PAIRS * H, LANES), F32)
    dma = pltpu.SemaphoreType.DMA
    anywhere = pl.BlockSpec(memory_space=pl.ANY)
    wanted = jnp.broadcast_to(corner_map.reshape(1, OWN), (8, OWN))
    shape = jax.ShapeDtypeStruct(rhs.shape, F32)
    return pl.pallas_call(
        kernel,
        out_shape=(shape, shape),
        in_specs=[anywhere, pl.BlockSpec(memory_space=pltpu.SMEM)] + [anywhere] * 5,
        out_specs=(anywhere, anywhere),
        scratch_shapes=[
            pltpu.VMEM((SUBS, 256, H), F32),
            pltpu.VMEM((SUBS, PS + 2 * NC, PS), BF16),
            pltpu.VMEM((SUBS, PS, PS), BF16),
            pltpu.VMEM((SUBS + 2, NC, PS), F32),
            pltpu.VMEM((256, NCO), F32),
            pltpu.VMEM((512, NCO), BF16),
            pltpu.VMEM((NGRP, 8, LANES), I32),
            pltpu.VMEM((2, 8, LANES), I32),
            pltpu.VMEM((NCO, 256), BF16),
            pltpu.VMEM((512, 512), BF16),
            pltpu.VMEM((2, NY, 256, 256), F32),
            pltpu.VMEM((NY, 512, 512), BF16),
            pltpu.VMEM((NY, NY, OWN, 256), F32),
            pltpu.VMEM((2, 2, OWN, 256), F32),
            pltpu.VMEM((2, NY, OWN, 256), F32),
            pltpu.VMEM((2 * OWN, NGRP * OWN), BF16),
            pltpu.VMEM((PAIRS, H, 8 * NC), BF16),
            pltpu.VMEM((PAIRS, H, LANES), F32),
            vector, vector, vector, vector, vector, vector, vector, vector, vector,
            pltpu.VMEM((CHUNKS, PAIRS * H, 2 * LANES), BF16),
            pltpu.VMEM((2, CHUNKS, SUBS, PS, LANES), F32),
            pltpu.VMEM((6, CHUNKS, H, LANES), F32),
            pltpu.VMEM((6, CHUNKS, H, LANES), F32),
            pltpu.VMEM((3, CHUNKS, NGRP, OWN, LANES), F32),
            pltpu.VMEM((3, CHUNKS, OWN, LANES), F32),
            pltpu.VMEM((3, CHUNKS, OWN + 2 * NC, LANES), F32),
            pltpu.VMEM((3, NGRP, CHUNKS, 8, LANES), F32),
            pltpu.VMEM((3, NSUB, CHUNKS, 8, LANES), F32),
            dma((14,)), dma((NGRP,)), dma((NGRP,)), dma((4,)), dma((4,)), dma((CHUNKS,)), dma((CHUNKS,)),
            dma((6, 2, CHUNKS)), dma((6, 2, CHUNKS)), dma((3, 2, CHUNKS)), dma((3, 2, CHUNKS)),
            dma((3, CHUNKS, 2 * NY - 1)), dma((3, CHUNKS, 2 * NY - 1)),
            dma((3, NGRP)), dma((3, NGRP)), dma((3, NSUB)), dma((3, NSUB)), dma((4,)), dma((4,)),
        ],
        compiler_params=pltpu.CompilerParams(
            collective_id=0, has_side_effects=True, vmem_limit_bytes=66_000_000
        ),
    )(rhs, counts, solve_panel, dirichlet_panel, coupling, wanted, coarse_inverse)


def solution(mesh):
    return jax.shard_map(
        local,
        mesh=mesh,
        in_specs=(
            P("grp", "sub", None, None),
            P("grp", "sub"),
            P("grp", "sub", None, None),
            P("grp", "sub", None, None),
            P("grp", "sub", None, None),
            P("grp", "sub", None),
            P("sub", "grp", None),
        ),
        out_specs=(P("grp", "sub", None, None), P("grp", "sub", None, None)),
        check_vma=False,
    )
```

time: 841 us -> 113 us (0.13)
  waiting for transfers between devices: 366 us -> 0 us
  blocking collectives: 348 us -> 0 us
  Pallas kernels: 0 us -> 107 us
  matrix products: 57.2 us -> 0 us
  starting transfers between devices: 25.7 us -> 0 us
  other arithmetic: 16.7 us -> 0 us
  between operations: 15.2 us -> 0.65 us
    psum x5 -> x0, blocking collectives: 348 us -> none  [the longest x3 206 us: residual_sum(): return lax.psum(inner(resid, precond), ('sub', 'grp'))]
    psum x3 -> x0, waiting for transfers between devices: 197 us -> none  [local(): solved = lax.psum(partial_solved, 'grp')]
    pallas_call x0 -> x1, Pallas kernels: none -> 107 us  [local(): pl.pallas_call(kernel, out_shape=(shape, shape), in_specs=[anywhere, pl.B...]
    reduce_scatter x3 -> x0, waiting for transfers between devices: 102 us -> none  [local(): lax.psum_scatter(jnp.einsum('skn,srk->nr', corner_onehot, corner_vals, pr...]
    ppermute x12 -> x0, waiting for transfers between devices: 66.6 us -> none  [passed_along(): return lax.ppermute(block, axis, route)]
    dot_general x21 -> x0, matrix products: 57.2 us -> none  [the longest x3 14.7 us: local(): jnp.einsum('mn,mr->nr', coarse_inverse[0], owned_totals, precision=HIGH)]
    ppermute x12 -> x0, starting transfers between devices: 25.1 us -> none  [passed_along(): return lax.ppermute(block, axis, route)]
  transfers between devices with their start and end apart: 18 -> 0, of which waited for: 18 -> 0; matrix products, arithmetic and copies ran while one was open for 0% -> 0% of each run, Pallas kernels for 0% -> 0%
where the time goes in v1:
time: 113 us; the launch traced here: 112 us
  Pallas kernels  107 us (95%)
  local copies, waits for them, and re-layouts  4.71 us (4%)
    pallas_call x1, Pallas kernels, local(): pl.pallas_call(kernel, out_shape=(shape, shape), in_specs=[anywhere, pl.B...  107 us
    unnamed x4, local copies, waits for them, and re-layouts  3.35 us

profile of v1, /device:TPU:1, one launch (start us, length us, event | category | flops | bytes accessed | tf_op | source)
XLA Modules:
  0.0 112.4 jit_solution(2664737304157885821)
XLA Ops:
  0.6 0.8 broadcast_in_dim.7
  1.4 0.6 broadcast_in_dim.8.map_h
  2.0 107.0 %shard_map.86 = (f32[1,4,256,256]{3,2,1,0:T(8,128)}, f32[1,4,256,256]{3,2,1,0:T(8,128)}) custom-call(f32[1,4,256,256]{3,2,1,0:T(8,128)} %rhs_h.1, s32[1,4]{1,0:T(1,128)} %counts_s.1, bf16[1,4,512,512]{3,2,1,0:T(8,128)(2,1)} %solve_h.1, bf16[1,4,512,512]{3,2,1,0:T(8,128)(2,1)} %dirichlet_h.1, f32[1,4,32,512]{3,2,1,0:T(8,128)} %coupling_h.1, ...), custom_call_target="tpu_custom_call" | custom-call | tf_op jit(solution)/shard_map/pallas_call | solution.py:553
  109.0 0.0 copy-start
  109.0 2.4 %copy.11 = f32[1,4,256,256]{3,2,1,0:T(8,128)} copy(f32[1,4,256,256]{3,2,1,0:T(8,128)} %get-tuple-element.4) | data formatting | bytes 2097152
  111.4 0.0 copy-done
  111.4 1.0 copy.12
Async XLA Ops:
  109.0 2.4 %copy-start = (f32[1,4,256,256]{3,2,1,0:T(8,128)S(1)}, f32[1,4,256,256]{3,2,1,0:T(8,128)}, u32[]{:S(2)}) copy-start(f32[1,4,256,256]{3,2,1,0:T(8,128)} %get-tuple-element.5) | copy-start | bytes 3145732

commit v2 on v1

v2 whole, which is shorter than its diff:
```python
import jax
import jax.numpy as jnp
from jax import lax
from jax.experimental import pallas as pl
from jax.experimental.pallas import tpu as pltpu
from jax.sharding import PartitionSpec as P

MESH = pl.DeviceIdType.MESH
F32, BF16, I32 = jnp.float32, jnp.bfloat16, jnp.int32
NSUB, NGRP, NY = 16, 8, 4
SUBS, H, PS, NC, NCO = 4, 256, 512, 32, 2048
LANES, CHUNKS, PAIRS = 128, 2, 5
OWN = SUBS * NC
LEFT, RIGHT = 0, 1


def remote(src, dst, send_sem, recv_sem, device):
    return pltpu.make_async_remote_copy(
        src_ref=src,
        dst_ref=dst,
        send_sem=send_sem,
        recv_sem=recv_sem,
        device_id=device,
        device_id_type=MESH,
    )


def split(value):
    high = value.astype(BF16)
    low = (value - high.astype(F32)).astype(BF16)
    return high, low


def colsum(value):
    return jnp.sum(value, axis=0, keepdims=True)


def chunks(body):
    for k in range(CHUNKS):
        body(k)


def block(i):
    return pl.ds(H * i, H)


def kernel(
    rhs_h, counts_s, solve_h, dirichlet_h, coupling_h, map_h, coarse_h, x_h, res_h,
    rhs_v, sc, dm, cext, ci, cis, cmt, cnt, onehot_a, onehot_b, rowhot, a_part, a_split, g_part, ring_a, ring_b,
    gs, ext, mask, r, u, w, m0, n0, m1, p, s, x, vs, wb, from_left, from_right, corners, cown, bext, red_a, red_b,
    load_sem, cm_send, cm_recv, misc_send, misc_recv, halo_send, halo_recv, ex_send, ex_recv,
    bk_send, bk_recv, ag_send, ag_recv, ra_send, ra_recv, rb_send, rb_recv, ring_send, ring_recv,
):
    sub, grp = lax.axis_index("sub"), lax.axis_index("grp")
    right, left = lax.rem(sub + 1, NSUB), lax.rem(sub + NSUB - 1, NSUB)
    y, core = lax.div(grp, 2), lax.rem(grp, 2)
    mate = 2 * y + 1 - core
    up, down, far = lax.rem(y + 1, NY), lax.rem(y + 3, NY), lax.rem(y + 2, NY)
    to_right, to_left, to_mate = {"sub": right}, {"sub": left}, {"grp": mate}
    to_up, to_down = {"grp": 2 * up + core}, {"grp": 2 * down + core}

    barrier = pltpu.get_barrier_semaphore()
    for i in range(1, NGRP):
        pl.semaphore_signal(barrier, inc=1, device_id={"grp": lax.rem(grp + i, NGRP)}, device_id_type=MESH)
    for i in range(1, NSUB):
        pl.semaphore_signal(barrier, inc=1, device_id={"sub": lax.rem(sub + i, NSUB)}, device_id_type=MESH)

    loads = [
        pltpu.make_async_copy(map_h.at[0], cmt.at[grp], load_sem.at[0]),
        pltpu.make_async_copy(rhs_h.at[0], rhs_v.at[pl.ds(1, SUBS)], load_sem.at[1]),
        pltpu.make_async_copy(coarse_h.at[0], ci, load_sem.at[2]),
        pltpu.make_async_copy(dirichlet_h.at[0], dm, load_sem.at[3]),
        pltpu.make_async_copy(coupling_h.at[0], cext.at[pl.ds(1, SUBS)], load_sem.at[4]),
        pltpu.make_async_copy(solve_h.at[0], sc.at[:, pl.ds(0, PS)], load_sem.at[5]),
    ]
    for load in loads:
        load.start()

    def map_copy(i):
        peer = lax.rem(grp + i, NGRP)
        return remote(map_h.at[0], cmt.at[grp], cm_send.at[i], cm_recv.at[i], {"grp": peer})

    def map_arrival(i):
        slot = lax.rem(grp + NGRP - i, NGRP)
        return remote(map_h.at[0], cmt.at[slot], cm_send.at[i], cm_recv.at[i], to_mate)

    count_copy = remote(cnt.at[0], cnt.at[1], misc_send.at[0], misc_recv.at[0], to_right)
    cpl_right = remote(
        coupling_h.at[0, SUBS - 1, :, pl.ds(H, H)], cext.at[0, :, pl.ds(H, H)],
        misc_send.at[1], misc_recv.at[1], to_right,
    )
    cpl_left = remote(
        coupling_h.at[0, 0, :, pl.ds(0, H)], cext.at[SUBS + 1, :, pl.ds(0, H)],
        misc_send.at[2], misc_recv.at[2], to_left,
    )
    mate_copy = remote(a_part.at[core], a_part.at[core], misc_send.at[3], misc_recv.at[3], to_mate)
    mate_arrival = remote(a_part.at[1 - core], a_part.at[1 - core], misc_send.at[3], misc_recv.at[3], to_mate)

    def ring(i, source, target, device):
        return remote(source, target, ring_send.at[i], ring_recv.at[i], device)

    front, rear = pl.ds(0, 2), pl.ds(2, 2)
    ring_copies = [
        ring(0, g_part.at[far, front], ring_a.at[0], to_up),
        ring(1, g_part.at[far, rear], ring_a.at[1], to_down),
        ring(2, g_part.at[up, rear], ring_b.at[0, rear], to_up),
        ring(3, g_part.at[down, front], ring_b.at[1, front], to_down),
        ring(4, g_part.at[up, front], ring_b.at[0, front], to_up),
        ring(5, g_part.at[down, rear], ring_b.at[1, rear], to_down),
    ]

    def halo_copy(k):
        part = pl.ds(LANES * k, LANES)
        return remote(
            rhs_h.at[0, SUBS - 1, part], rhs_v.at[0, part], halo_send.at[k], halo_recv.at[k], to_right
        )

    def face_left(op, k):
        return remote(
            wb.at[op % 2, k, 0, pl.ds(0, H)], from_right.at[op, k],
            ex_send.at[op, LEFT, k], ex_recv.at[op, LEFT, k], to_left,
        )

    def face_right(op, k):
        return remote(
            wb.at[op % 2, k, SUBS - 1, pl.ds(H, H)], from_left.at[op, k],
            ex_send.at[op, RIGHT, k], ex_recv.at[op, RIGHT, k], to_right,
        )

    def back_left(f, k):
        return remote(
            bext.at[f, k, pl.ds(NC, NC)], bext.at[f, k, pl.ds(NC + OWN, NC)],
            bk_send.at[f, LEFT, k], bk_recv.at[f, LEFT, k], to_left,
        )

    def back_right(f, k):
        return remote(
            bext.at[f, k, pl.ds(OWN, NC)], bext.at[f, k, pl.ds(0, NC)],
            bk_send.at[f, RIGHT, k], bk_recv.at[f, RIGHT, k], to_right,
        )

    def corner_link(f, k, i, part, device):
        return remote(part, part, ag_send.at[f, k, i], ag_recv.at[f, k, i], device)

    def corner_slot(f, k, chip, mine=True):
        return corners.at[f, k, 2 * chip + (core if mine else 1 - core)]

    half_a, half_b = pl.ds(0, OWN // 2), pl.ds(OWN // 2, OWN // 2)

    def corner_sends(f, k):
        own = corner_slot(f, k, y)
        return [corner_link(f, k, i, own, to) for i, to in enumerate((to_mate, to_up, to_down))]

    def corner_near(f, k):
        return [
            corner_link(f, k, 1, corner_slot(f, k, down), to_up),
            corner_link(f, k, 2, corner_slot(f, k, up), to_down),
        ]

    def corner_relays(f, k):
        return [
            corner_link(f, k, 3, corner_slot(f, k, down).at[half_a], to_up),
            corner_link(f, k, 4, corner_slot(f, k, up).at[half_b], to_down),
        ]

    def corner_far(f, k):
        return [
            corner_link(f, k, 3, corner_slot(f, k, far).at[half_a], to_up),
            corner_link(f, k, 4, corner_slot(f, k, far).at[half_b], to_down),
        ]

    def corner_forwards(f, k, mine=True):
        return [
            corner_link(f, k, 5, corner_slot(f, k, down, mine), to_mate),
            corner_link(f, k, 6, corner_slot(f, k, up, mine), to_mate),
            corner_link(f, k, 7, corner_slot(f, k, far, mine).at[half_a], to_mate),
            corner_link(f, k, 8, corner_slot(f, k, far, mine).at[half_b], to_mate),
        ]

    def corner_mate(f, k):
        return corner_link(f, k, 0, corner_slot(f, k, y, False), to_mate)

    def sum_a(t, i):
        mine = red_a.at[t, grp]
        return remote(mine, mine, ra_send.at[t, i], ra_recv.at[t, i], {"grp": lax.rem(grp + i, NGRP)})

    def sum_a_arrival(t, i):
        there = red_a.at[t, lax.rem(grp + NGRP - i, NGRP)]
        return remote(there, there, ra_send.at[t, i], ra_recv.at[t, i], to_mate)

    def sum_b(t, i):
        mine = red_b.at[t, sub]
        return remote(mine, mine, rb_send.at[t, i], rb_recv.at[t, i], {"sub": lax.rem(sub + i, NSUB)})

    def sum_b_arrival(t, i):
        there = red_b.at[t, lax.rem(sub + NSUB - i, NSUB)]
        return remote(there, there, rb_send.at[t, i], rb_recv.at[t, i], to_right)


    def split_vector(vector, k, pairs):
        for i in pairs:
            high, low = split(vector[k, block(i)])
            vs[k, block(i), pl.ds(0, LANES)] = high
            vs[k, block(i), pl.ds(LANES, LANES)] = low

    def apply_panel(op, k, j):
        solve = op % 2 == 1
        faces = vs[k, pl.ds(H * j, PS), :]
        both = jnp.dot((sc if solve else dm)[j], faces, preferred_element_type=F32)
        both = both[:, :LANES] + both[:, LANES:]
        wb[op % 2, k, j] = both[:PS]
        if solve:
            f = op // 2
            values = both[PS : PS + NC] + both[PS + NC :]
            cown[f, k, pl.ds(NC * j, NC)] = values
            corners[f, k, grp, pl.ds(NC * j, NC)] = values

    def start(op, k, vector, last=False):
        solve = op % 2 == 1
        if op >= 2:
            face_left(op - 2, k).wait_send()
            face_right(op - 2, k).wait_send()
        split_vector(vector, k, range(PAIRS))
        apply_panel(op, k, 0)
        face_left(op, k).start()
        apply_panel(op, k, SUBS - 1)
        if not last:
            face_right(op, k).start()
        apply_panel(op, k, 1)
        apply_panel(op, k, 2)
        if solve:
            for copy in corner_sends(op // 2, k):
                copy.start()

    def gather_near(f, k):
        near, relays, forwards = corner_near(f, k), corner_relays(f, k), corner_forwards(f, k)
        for i in range(2):
            near[i].wait_recv()
            relays[i].start()
            forwards[i].start()

    def gather_far(f, k):
        arrivals, forwards = corner_far(f, k), corner_forwards(f, k)
        for i in range(2):
            arrivals[i].wait_recv()
            forwards[2 + i].start()

    def coarse(f, k, last=False):
        corner_mate(f, k).wait_recv()
        for copy in corner_forwards(f, k, False):
            copy.wait_recv()
        high, low = split(corners[f, k].reshape(NGRP * OWN, LANES))
        both = jnp.dot(gs[...], jnp.concatenate([high, low], axis=1), preferred_element_type=F32)
        both = both[:, :LANES] + both[:, LANES:]
        bext[f, k, pl.ds(NC, OWN)] = both[:OWN] + both[OWN:]
        back_left(f, k).start()
        if not last:
            back_right(f, k).start()

    def all_coarse(f, last=False):
        chunks(lambda k: gather_near(f, k))
        chunks(lambda k: gather_far(f, k))
        chunks(lambda k: coarse(f, k, last))

    def image(op, k, i):
        before = from_left[op, k] if i == 0 else wb[op % 2, k, i - 1, pl.ds(H, H)]
        after = from_right[op, k] if i == SUBS else wb[op % 2, k, i, pl.ds(0, H)]
        value = before + after
        if op % 2 == 1:
            high, low = split(bext[op // 2, k, pl.ds(NC * i, 2 * NC)])
            faces = jnp.concatenate([high, low, high, low], axis=0)
            value = value + jnp.dot(ext[i], faces, preferred_element_type=F32)
        else:
            value = 0.25 * value
        return jnp.where(mask[i] > 0.0, value, 0.0)

    def arrive(op, k, last=False):
        face_left(op, k).wait_recv()
        if op % 2 == 1:
            back_left(op // 2, k).wait_recv()
        if not last:
            face_right(op, k).wait_recv()
            if op % 2 == 1:
                back_right(op // 2, k).wait_recv()

    def finish(op, k, out):
        for i in range(1, SUBS):
            if op % 2 == 0:
                out[k, block(i)] = image(op, k, i)
        arrive(op, k)
        for i in (0, SUBS) if op % 2 == 0 else range(PAIRS):
            out[k, block(i)] = image(op, k, i)

    def product(first, second, k):
        return colsum(first[k, pl.ds(H, SUBS * H)] * second[k, pl.ds(H, SUBS * H)])

    def put_sums(t, k, values):
        for i, value in enumerate(values):
            red_a[t, grp, pl.ds(3 * k + i, 1)] = value

    def send_sums(t):
        for i in range(1, NGRP):
            sum_a(t, i).start()

    def pass_sums(t):
        for i in range(1, NGRP):
            sum_a_arrival(t, i).wait_recv()
        red_b[t, sub] = jnp.sum(red_a[t], axis=0)
        for i in range(1, NSUB):
            sum_b(t, i).start()

    def get_sums(t):
        for i in range(1, NSUB):
            sum_b_arrival(t, i).wait_recv()
        total = jnp.sum(red_b[t], axis=0)
        return [[total[3 * k + i : 3 * k + i + 1] for i in range(3)] for k in range(CHUNKS)]

    live = [counts_s[0, c] for c in range(SUBS)]
    live[SUBS - 1] = jnp.where(sub == NSUB - 1, 0, live[SUBS - 1])
    cnt[0] = jnp.full((8, LANES), live[SUBS - 1], I32)
    red_a[...] = jnp.zeros_like(red_a)
    pl.semaphore_wait(barrier, NGRP + NSUB - 2)
    for i in range(1, NGRP):
        map_copy(i).start()
    count_copy.start()
    chunks(lambda k: halo_copy(k).start())
    cpl_right.start()
    cpl_left.start()

    loads[2].wait()
    for i in range(4):
        high, low = split(ci[pl.ds(64 * i, 64)])
        cis[pl.ds(64 * i, 64)] = high
        cis[pl.ds(256 + 64 * i, 64)] = low
    rows = lax.broadcasted_iota(I32, (H, LANES), 0)
    for c in range(SUBS):
        mask[c + 1] = (rows < live[c]).astype(F32)
    loads[1].wait()
    for c in range(SUBS):
        turned = rhs_v[c + 1].T
        for k in range(CHUNKS):
            r[k, block(c + 1)] = jnp.where(
                mask[c + 1] > 0.0, turned[:, LANES * k : LANES * (k + 1)], 0.0
            )

    loads[0].wait()
    for i in range(1, NGRP):
        map_arrival(i).wait_recv()

    def map_row(g):
        return jnp.concatenate([cmt[g, pl.ds(c, 1)] for c in range(SUBS)], axis=1)

    def fill(onehot, q):
        for c in range(2):
            wanted = map_row(2 * q + c)
            for t in range(NCO // 256):
                hit = rows + 256 * t == wanted
                onehot[pl.ds(256 * t, 256), pl.ds(LANES * c, LANES)] = hit.astype(F32).astype(BF16)

    slots = (onehot_a, onehot_b)
    fill(onehot_a, 0)
    for q in range(NY):
        if q + 1 < NY:
            fill(slots[(q + 1) % 2], q + 1)
        both = jnp.dot(cis[...], slots[q % 2][...], preferred_element_type=F32)
        a_part[core, q] = both[:256] + both[256:]
    mate_copy.start()

    loads[3].wait()
    for j in range(SUBS):
        for a, b in ((0, 1), (1, 0)):
            dm[j, block(a), block(b)] = -dm[j, block(a), block(b)]
    count_copy.wait_recv()
    mask[0] = (rows < cnt[1, pl.ds(0, 1)]).astype(F32)

    def first(k):
        halo_copy(k).wait_recv()
        r[k, block(0)] = jnp.where(mask[0] > 0.0, rhs_v[0, pl.ds(LANES * k, LANES)].T, 0.0)
        start(0, k, r)

    chunks(first)

    mate_arrival.wait_recv()
    for q in range(NY):
        for c in range(2):
            high, low = split(a_part[c, q])
            a_split[q, block(c), pl.ds(0, 256)] = high
            a_split[q, block(c), pl.ds(256, 256)] = low
    lane = lax.broadcasted_iota(I32, (LANES, LANES), 1).astype(F32)
    base = (2 * 256 * y).astype(F32)
    for q in range(NY):
        wanted = jnp.broadcast_to(map_row(2 * q + core), (LANES, LANES)).astype(F32).T
        for t in range(4):
            rowhot[pl.ds(LANES * q, LANES), pl.ds(LANES * t, LANES)] = (
                wanted == lane + (base + 128.0 * t)
            ).astype(F32).astype(BF16)
    for q in range(NY):
        both = jnp.dot(rowhot[...], a_split[q], preferred_element_type=F32)
        both = both[:, :256] + both[:, 256:]
        for chip in range(NY):
            g_part[chip, q] = both[LANES * chip : LANES * (chip + 1)]
    for i in range(4):
        ring_copies[i].start()

    loads[5].wait()
    loads[4].wait()
    cpl_right.wait_recv()
    cpl_left.wait_recv()
    for j in range(SUBS):
        for a, b in ((0, 1), (1, 0)):
            sc[j, block(a), block(b)] = -sc[j, block(a), block(b)]
        for half in range(2):
            part = cext[j + 1, :, block(half)]
            high, low = split(part if half else -part)
            sc[j, pl.ds(PS, NC), block(half)] = high
            sc[j, pl.ds(PS + NC, NC), block(half)] = low

    def second(k):
        finish(0, k, u)
        start(1, k, u)

    chunks(second)
    ring_copies[0].wait_recv()
    g_part[up, front] = g_part[up, front] + ring_a[0]
    ring_copies[4].start()
    ring_copies[1].wait_recv()
    g_part[down, rear] = g_part[down, rear] + ring_a[1]
    ring_copies[5].start()
    chunks(lambda k: gather_near(0, k))
    for i in range(PAIRS):
        both = jnp.concatenate([cext[i, :, block(1)], -cext[i + 1, :, block(0)]], axis=0)
        high = both.astype(BF16).astype(F32)
        low = both - high
        ext[i] = jnp.concatenate([high, high, low, low], axis=0).T.astype(BF16)
    chunks(lambda k: gather_far(0, k))
    for i in range(2, 6):
        ring_copies[i].wait_recv()
    for q in range(NY):
        high, low = split(g_part[y, q] + ring_b[0, q] + ring_b[1, q])
        gs[pl.ds(0, OWN), pl.ds(256 * q, 256)] = high
        gs[pl.ds(OWN, OWN), pl.ds(256 * q, 256)] = low

    chunks(lambda k: coarse(0, k))

    def third(k):
        finish(1, k, w)
        start(2, k, w)
        put_sums(0, k, [product(r, u, k), product(u, w, k)])

    chunks(third)
    send_sums(0)

    def fourth(k):
        finish(2, k, m0)
        start(3, k, m0)

    chunks(fourth)
    pass_sums(0)
    all_coarse(1)
    rz0, den0, alpha0 = [], [], []
    for rz, uw, _ in get_sums(0):
        rz0.append(rz)
        den0.append(uw)
        alpha0.append(rz / uw)

    def fifth(k):
        arrive(3, k)
        for i in range(PAIRS):
            here = (k, block(i))
            s[here] = w[here]
            n0[here] = image(3, k, i)
            w[here] = w[here] - alpha0[k] * n0[here]
        start(4, k, w)
        for i in range(PAIRS):
            here = (k, block(i))
            p[here] = u[here]
            x[here] = alpha0[k] * u[here]
            r[here] = r[here] - alpha0[k] * s[here]
            u[here] = u[here] - alpha0[k] * m0[here]
        put_sums(1, k, [product(r, u, k), product(u, w, k), product(u, s, k)])

    chunks(fifth)
    send_sums(1)

    def sixth(k):
        finish(4, k, m1)
        start(5, k, m1, last=True)

    chunks(sixth)
    pass_sums(1)
    chunks(lambda k: gather_near(2, k))
    rz1, den1, alpha1 = [], [], []
    beta1 = []
    for k, (rz, uw, us) in enumerate(get_sums(1)):
        beta = rz / rz0[k]
        den = uw + beta * (us + us) + beta * beta * den0[k]
        rz1.append(rz)
        den1.append(den)
        beta1.append(beta)
        alpha1.append(rz / den)
    chunks(lambda k: gather_far(2, k))

    partial = []

    def seventh(k):
        alpha, beta = alpha1[k], beta1[k]
        for i in range(PAIRS):
            here = (k, block(i))
            p[here] = u[here] + beta * p[here]
            s[here] = w[here] + beta * s[here]
            x[here] = x[here] + alpha * p[here]
            r[here] = r[here] - alpha * s[here]
            u[here] = u[here] - alpha * (m1[here] + beta * m0[here])
            w[here] = w[here] - (alpha * beta) * n0[here]
        faces = jnp.zeros((1, LANES), F32)
        for j in range(SUBS):
            faces = faces + colsum(u[k, pl.ds(H * j, PS)] * wb[1, k, j])
        partial.append([product(r, u, k), product(u, w, k), product(u, s, k), faces])

    chunks(seventh)
    chunks(lambda k: coarse(2, k, last=True))
    for k in range(CHUNKS):
        corner = cown[0, k] - alpha0[k] * cown[1, k] - alpha1[k] * (cown[2, k] + beta1[k] * cown[1, k])
        ru, uw, us, faces = partial[k]
        faces = faces + colsum(corner * bext[2, k, pl.ds(NC, OWN)])
        put_sums(2, k, [ru, uw - alpha1[k] * faces, us])
    send_sums(2)

    for i in range(1, NGRP):
        map_copy(i).wait_send()
    for copy in (count_copy, cpl_right, cpl_left, mate_copy, *ring_copies):
        copy.wait_send()
    for t in range(2):
        for i in range(1, NGRP):
            sum_a(t, i).wait_send()
    pass_sums(2)

    def under(k):
        arrive(5, k, last=True)
        for i in range(1, PAIRS):
            here = (k, block(i))
            w[here] = w[here] - alpha1[k] * image(5, k, i)

    chunks(under)

    def drain(k):
        halo_copy(k).wait_send()
        face_left(4, k).wait_send()
        face_right(4, k).wait_send()
        face_left(5, k).wait_send()
        for f in range(3):
            back_left(f, k).wait_send()
            if f < 2:
                back_right(f, k).wait_send()
            for copy in corner_sends(f, k) + corner_relays(f, k) + corner_forwards(f, k):
                copy.wait_send()

    chunks(drain)
    for t in range(2):
        for i in range(1, NSUB):
            sum_b(t, i).wait_send()
    for i in range(1, NGRP):
        sum_a(2, i).wait_send()

    stores = []
    for k, (rz, uw, us) in enumerate(get_sums(2)):
        beta = rz / rz1[k]
        den = uw + beta * (us + us) + beta * beta * den1[k]
        alpha = rz / den
        for i in range(1, PAIRS):
            here = (k, block(i))
            x[here] = x[here] + alpha * (u[here] + beta * p[here])
            r[here] = r[here] - alpha * (w[here] + beta * s[here])
        own = (k, pl.ds(H, SUBS * H))
        stores.append(pltpu.make_async_copy(x.at[own], x_h.at[k], load_sem.at[6 + 2 * k]))
        stores.append(pltpu.make_async_copy(r.at[own], res_h.at[k], load_sem.at[7 + 2 * k]))
        stores[-2].start()
        stores[-1].start()
    for i in range(1, NSUB):
        sum_b(2, i).wait_send()
    for copy in stores:
        copy.wait()


def turn(x_ref, r_ref, x_out, r_out):
    for source, target in ((x_ref, x_out), (r_ref, r_out)):
        for k in range(CHUNKS):
            target[0, 0, pl.ds(LANES * k, LANES)] = source[k].T


def local(rhs, counts, solve_panel, dirichlet_panel, coupling, corner_map, coarse_inverse):
    vector = pltpu.VMEM((CHUNKS, PAIRS * H, LANES), F32)
    dma = pltpu.SemaphoreType.DMA
    anywhere = pl.BlockSpec(memory_space=pl.ANY)
    shape = jax.ShapeDtypeStruct((CHUNKS, SUBS * H, LANES), F32)
    x_turned, r_turned = pl.pallas_call(
        kernel,
        out_shape=(shape, shape),
        in_specs=[anywhere, pl.BlockSpec(memory_space=pltpu.SMEM)] + [anywhere] * 5,
        out_specs=(anywhere, anywhere),
        scratch_shapes=[
            pltpu.VMEM((PAIRS, 256, H), F32),
            pltpu.VMEM((SUBS, PS + 2 * NC, PS), BF16),
            pltpu.VMEM((SUBS, PS, PS), BF16),
            pltpu.VMEM((SUBS + 2, NC, PS), F32),
            pltpu.VMEM((256, NCO), F32),
            pltpu.VMEM((512, NCO), BF16),
            pltpu.VMEM((NGRP, SUBS, NC), I32),
            pltpu.VMEM((2, 8, LANES), I32),
            pltpu.VMEM((NCO, 256), BF16),
            pltpu.VMEM((NCO, 256), BF16),
            pltpu.VMEM((512, 512), BF16),
            pltpu.VMEM((2, NY, 256, 256), F32),
            pltpu.VMEM((NY, 512, 512), BF16),
            pltpu.VMEM((NY, NY, OWN, 256), F32),
            pltpu.VMEM((2, 2, OWN, 256), F32),
            pltpu.VMEM((2, NY, OWN, 256), F32),
            pltpu.VMEM((2 * OWN, NGRP * OWN), BF16),
            pltpu.VMEM((PAIRS, H, 8 * NC), BF16),
            pltpu.VMEM((PAIRS, H, LANES), F32),
            vector, vector, vector, vector, vector, vector, vector, vector, vector,
            pltpu.VMEM((CHUNKS, PAIRS * H, 2 * LANES), BF16),
            pltpu.VMEM((2, CHUNKS, SUBS, PS, LANES), F32),
            pltpu.VMEM((6, CHUNKS, H, LANES), F32),
            pltpu.VMEM((6, CHUNKS, H, LANES), F32),
            pltpu.VMEM((3, CHUNKS, NGRP, OWN, LANES), F32),
            pltpu.VMEM((3, CHUNKS, OWN, LANES), F32),
            pltpu.VMEM((3, CHUNKS, OWN + 2 * NC, LANES), F32),
            pltpu.VMEM((3, NGRP, 8, LANES), F32),
            pltpu.VMEM((3, NSUB, 8, LANES), F32),
            dma((10,)), dma((NGRP,)), dma((NGRP,)), dma((4,)), dma((4,)), dma((CHUNKS,)), dma((CHUNKS,)),
            dma((6, 2, CHUNKS)), dma((6, 2, CHUNKS)), dma((3, 2, CHUNKS)), dma((3, 2, CHUNKS)),
            dma((3, CHUNKS, 9)), dma((3, CHUNKS, 9)),
            dma((3, NGRP)), dma((3, NGRP)), dma((3, NSUB)), dma((3, NSUB)), dma((6,)), dma((6,)),
        ],
        compiler_params=pltpu.CompilerParams(
            collective_id=0, has_side_effects=True, vmem_limit_bytes=66_000_000
        ),
    )(rhs, counts, solve_panel, dirichlet_panel, coupling, corner_map, coarse_inverse)
    out = jax.ShapeDtypeStruct(rhs.shape, F32)
    taken = pl.BlockSpec((CHUNKS, H, LANES), lambda c: (0, c, 0))
    given = pl.BlockSpec((1, 1, CHUNKS * LANES, H), lambda c: (0, c, 0, 0))
    return pl.pallas_call(
        turn,
        out_shape=(out, out),
        grid=(SUBS,),
        in_specs=[taken, taken],
        out_specs=(given, given),
    )(x_turned, r_turned)


def solution(mesh):
    return jax.shard_map(
        local,
        mesh=mesh,
        in_specs=(
            P("grp", "sub", None, None),
            P("grp", "sub"),
            P("grp", "sub", None, None),
            P("grp", "sub", None, None),
            P("grp", "sub", None, None),
            P("grp", "sub", None),
            P("sub", "grp", None),
        ),
        out_specs=(P("grp", "sub", None, None), P("grp", "sub", None, None)),
        check_vma=False,
    )
```

time: 113 us -> 112 us (level)
  local copies, waits for them, and re-layouts: 4.71 us -> 0 us
  Pallas kernels: 107 us -> 111 us
    pallas_call x0 -> x1, Pallas kernels: none -> 3.96 us  [local(): pl.pallas_call(turn, out_shape=(out, out), grid=(SUBS,), in_specs=[taken,...]
    unnamed x4 -> x0, local copies, waits for them, and re-layouts: 3.35 us -> none
    broadcast_in_dim x2 -> x0, local copies, waits for them, and re-layouts: 1.36 us -> none  [local(): wanted = jnp.broadcast_to(corner_map.reshape(1, OWN), (8, OWN))]
where the time goes in v2:
time: 112 us
  Pallas kernels  111 us (99%)
    pallas_call x1, Pallas kernels, local(): pl.pallas_call(kernel, out_shape=(shape, shape), in_specs=[anywhere, pl.B...  107 us
    pallas_call x1, Pallas kernels, local(): pl.pallas_call(turn, out_shape=(out, out), grid=(SUBS,), in_specs=[taken,...  3.96 us

profile of v2, /device:TPU:1, one launch (start us, length us, event | category | flops | bytes accessed | tf_op | source)
XLA Modules:
  0.0 111.6 jit_solution(454151385999981428)
XLA Ops:
  0.6 107.0 %shard_map.86 = (f32[2,1024,128]{2,1,0:T(8,128)}, f32[2,1024,128]{2,1,0:T(8,128)}) custom-call(f32[1,4,256,256]{3,2,1,0:T(8,128)} %rhs_h.1, s32[1,4]{1,0:T(1,128)} %counts_s.1, bf16[1,4,512,512]{3,2,1,0:T(8,128)(2,1)} %solve_h.1, bf16[1,4,512,512]{3,2,1,0:T(8,128)(2,1)} %dirichlet_h.1, f32[1,4,32,512]{3,2,1,0:T(8,128)} %coupling_h.1, s32[1,4,32]{2,1,0:T(4,128)} %map_h.1, ...), custom_call_target="tpu_custom_call" | custom-call | tf_op jit(solution)/shard_map/pallas_call | solution.py:596
  107.6 4.0 %shard_map.87 = (f32[1,4,256,256]{3,2,1,0:T(8,128)}, f32[1,4,256,256]{3,2,1,0:T(8,128)}) custom-call(f32[2,1024,128]{2,1,0:T(8,128)} %get-tuple-element.4.x_ref, f32[2,1024,128]{2,1,0:T(8,128)} %get-tuple-element.5.r_ref), custom_call_target="tpu_custom_call" | custom-call | tf_op jit(solution)/shard_map/pallas_call | solution.py:643

commit v3 on v2

--- a/solution.py
+++ b/solution.py
@@ -93,8 +93,10 @@
         coupling_h.at[0, 0, :, pl.ds(0, H)], cext.at[SUBS + 1, :, pl.ds(0, H)],
         misc_send.at[2], misc_recv.at[2], to_left,
     )
-    mate_copy = remote(a_part.at[core], a_part.at[core], misc_send.at[3], misc_recv.at[3], to_mate)
-    mate_arrival = remote(a_part.at[1 - core], a_part.at[1 - core], misc_send.at[3], misc_recv.at[3], to_mate)
+
+    def mate_copy(q, mine=True):
+        part = a_part.at[core if mine else 1 - core, q]
+        return remote(part, part, misc_send.at[3 + q], misc_recv.at[3 + q], to_mate)
 
     def ring(i, source, target, device):
         return remote(source, target, ring_send.at[i], ring_recv.at[i], device)
@@ -145,40 +147,15 @@
     def corner_slot(f, k, chip, mine=True):
         return corners.at[f, k, 2 * chip + (core if mine else 1 - core)]
 
-    half_a, half_b = pl.ds(0, OWN // 2), pl.ds(OWN // 2, OWN // 2)
-
-    def corner_sends(f, k):
-        own = corner_slot(f, k, y)
-        return [corner_link(f, k, i, own, to) for i, to in enumerate((to_mate, to_up, to_down))]
-
-    def corner_near(f, k):
-        return [
-            corner_link(f, k, 1, corner_slot(f, k, down), to_up),
-            corner_link(f, k, 2, corner_slot(f, k, up), to_down),
-        ]
-
-    def corner_relays(f, k):
-        return [
-            corner_link(f, k, 3, corner_slot(f, k, down).at[half_a], to_up),
-            corner_link(f, k, 4, corner_slot(f, k, up).at[half_b], to_down),
-        ]
-
-    def corner_far(f, k):
-        return [
-            corner_link(f, k, 3, corner_slot(f, k, far).at[half_a], to_up),
-            corner_link(f, k, 4, corner_slot(f, k, far).at[half_b], to_down),
-        ]
-
-    def corner_forwards(f, k, mine=True):
-        return [
-            corner_link(f, k, 5, corner_slot(f, k, down, mine), to_mate),
-            corner_link(f, k, 6, corner_slot(f, k, up, mine), to_mate),
-            corner_link(f, k, 7, corner_slot(f, k, far, mine).at[half_a], to_mate),
-            corner_link(f, k, 8, corner_slot(f, k, far, mine).at[half_b], to_mate),
-        ]
-
-    def corner_mate(f, k):
-        return corner_link(f, k, 0, corner_slot(f, k, y, False), to_mate)
+    def corner_copy(f, k, i):
+        device = to_mate if i == 0 else {"grp": 2 * lax.rem(y + i, NY) + core}
+        return corner_link(f, k, i, corner_slot(f, k, y), device)
+
+    def corner_arrival(f, k, i):
+        return corner_link(f, k, i, corner_slot(f, k, lax.rem(y + NY - i, NY), i > 0), to_mate)
+
+    def corner_forward(f, k, i, mine=True):
+        return corner_link(f, k, NY - 1 + i, corner_slot(f, k, lax.rem(y + NY - i, NY), mine), to_mate)
 
     def sum_a(t, i):
         mine = red_a.at[t, grp]
@@ -196,12 +173,6 @@
         there = red_b.at[t, lax.rem(sub + NSUB - i, NSUB)]
         return remote(there, there, rb_send.at[t, i], rb_recv.at[t, i], to_right)
 
-
-    def split_vector(vector, k, pairs):
-        for i in pairs:
-            high, low = split(vector[k, block(i)])
-            vs[k, block(i), pl.ds(0, LANES)] = high
-            vs[k, block(i), pl.ds(LANES, LANES)] = low
 
     def apply_panel(op, k, j):
         solve = op % 2 == 1
@@ -215,40 +186,44 @@
             cown[f, k, pl.ds(NC * j, NC)] = values
             corners[f, k, grp, pl.ds(NC * j, NC)] = values
 
-    def start(op, k, vector, last=False):
-        solve = op % 2 == 1
-        if op >= 2:
-            face_left(op - 2, k).wait_send()
-            face_right(op - 2, k).wait_send()
-        split_vector(vector, k, range(PAIRS))
-        apply_panel(op, k, 0)
-        face_left(op, k).start()
-        apply_panel(op, k, SUBS - 1)
-        if not last:
-            face_right(op, k).start()
-        apply_panel(op, k, 1)
-        apply_panel(op, k, 2)
-        if solve:
-            for copy in corner_sends(op // 2, k):
-                copy.start()
-
-    def gather_near(f, k):
-        near, relays, forwards = corner_near(f, k), corner_relays(f, k), corner_forwards(f, k)
-        for i in range(2):
-            near[i].wait_recv()
-            relays[i].start()
-            forwards[i].start()
-
-    def gather_far(f, k):
-        arrivals, forwards = corner_far(f, k), corner_forwards(f, k)
-        for i in range(2):
-            arrivals[i].wait_recv()
-            forwards[2 + i].start()
+    def put_faces(k, pairs, value):
+        for i in pairs:
+            high, low = split(value(k, i))
+            vs[k, block(i), pl.ds(0, LANES)] = high
+            vs[k, block(i), pl.ds(LANES, LANES)] = low
+
+    def inner(op, value):
+        for k in range(CHUNKS):
+            put_faces(k, range(1, SUBS), value)
+            apply_panel(op, k, 1)
+            apply_panel(op, k, 2)
+
+    def outer(op, value, last=False):
+        for k in range(CHUNKS):
+            if op > 0:
+                arrive(op - 1, k)
+            if op >= 2:
+                face_left(op - 2, k).wait_send()
+                face_right(op - 2, k).wait_send()
+            put_faces(k, (0, SUBS), value)
+            apply_panel(op, k, 0)
+            face_left(op, k).start()
+            apply_panel(op, k, SUBS - 1)
+            if op % 2 == 1:
+                for i in (2, 1, 3, 0):
+                    corner_copy(op // 2, k, i).start()
+            if not last:
+                face_right(op, k).start()
+
+    def gather(f, k):
+        for i in (1, 3, 2):
+            corner_arrival(f, k, i).wait_recv()
+            corner_forward(f, k, i).start()
 
     def coarse(f, k, last=False):
-        corner_mate(f, k).wait_recv()
-        for copy in corner_forwards(f, k, False):
-            copy.wait_recv()
+        corner_arrival(f, k, 0).wait_recv()
+        for i in range(1, NY):
+            corner_forward(f, k, i, False).wait_recv()
         high, low = split(corners[f, k].reshape(NGRP * OWN, LANES))
         both = jnp.dot(gs[...], jnp.concatenate([high, low], axis=1), preferred_element_type=F32)
         both = both[:, :LANES] + both[:, LANES:]
@@ -258,9 +233,10 @@
             back_right(f, k).start()
 
     def all_coarse(f, last=False):
-        chunks(lambda k: gather_near(f, k))
-        chunks(lambda k: gather_far(f, k))
-        chunks(lambda k: coarse(f, k, last))
+        for k in range(CHUNKS):
+            gather(f, k)
+        for k in range(CHUNKS):
+            coarse(f, k, last)
 
     def image(op, k, i):
         before = from_left[op, k] if i == 0 else wb[op % 2, k, i - 1, pl.ds(H, H)]
@@ -283,13 +259,13 @@
             if op % 2 == 1:
                 back_right(op // 2, k).wait_recv()
 
-    def finish(op, k, out):
-        for i in range(1, SUBS):
-            if op % 2 == 0:
-                out[k, block(i)] = image(op, k, i)
-        arrive(op, k)
-        for i in (0, SUBS) if op % 2 == 0 else range(PAIRS):
-            out[k, block(i)] = image(op, k, i)
+    def image_in(op, out):
+        def value(k, i):
+            result = image(op, k, i)
+            out[k, block(i)] = result
+            return result
+
+        return value
 
     def product(first, second, k):
         return colsum(first[k, pl.ds(H, SUBS * H)] * second[k, pl.ds(H, SUBS * H)])
@@ -343,6 +319,20 @@
                 mask[c + 1] > 0.0, turned[:, LANES * k : LANES * (k + 1)], 0.0
             )
 
+    loads[3].wait()
+    for j in range(SUBS):
+        for a, b in ((0, 1), (1, 0)):
+            dm[j, block(a), block(b)] = -dm[j, block(a), block(b)]
+
+    def residual(k, i):
+        if i == 0:
+            halo_copy(k).wait_recv()
+            turned = rhs_v[0, pl.ds(LANES * k, LANES)].T
+            r[k, block(0)] = jnp.where(mask[0] > 0.0, turned, 0.0)
+        return r[k, block(i)]
+
+    inner(0, residual)
+
     loads[0].wait()
     for i in range(1, NGRP):
         map_arrival(i).wait_recv()
@@ -364,24 +354,14 @@
             fill(slots[(q + 1) % 2], q + 1)
         both = jnp.dot(cis[...], slots[q % 2][...], preferred_element_type=F32)
         a_part[core, q] = both[:256] + both[256:]
-    mate_copy.start()
-
-    loads[3].wait()
-    for j in range(SUBS):
-        for a, b in ((0, 1), (1, 0)):
-            dm[j, block(a), block(b)] = -dm[j, block(a), block(b)]
+        mate_copy(q).start()
+
     count_copy.wait_recv()
     mask[0] = (rows < cnt[1, pl.ds(0, 1)]).astype(F32)
-
-    def first(k):
-        halo_copy(k).wait_recv()
-        r[k, block(0)] = jnp.where(mask[0] > 0.0, rhs_v[0, pl.ds(LANES * k, LANES)].T, 0.0)
-        start(0, k, r)
-
-    chunks(first)
-
-    mate_arrival.wait_recv()
+    outer(0, residual)
+
     for q in range(NY):
+        mate_copy(q, False).wait_recv()
         for c in range(2):
             high, low = split(a_part[c, q])
             a_split[q, block(c), pl.ds(0, 256)] = high
@@ -415,24 +395,20 @@
             sc[j, pl.ds(PS, NC), block(half)] = high
             sc[j, pl.ds(PS + NC, NC), block(half)] = low
 
-    def second(k):
-        finish(0, k, u)
-        start(1, k, u)
-
-    chunks(second)
+    inner(1, image_in(0, u))
+    outer(1, image_in(0, u))
     ring_copies[0].wait_recv()
     g_part[up, front] = g_part[up, front] + ring_a[0]
     ring_copies[4].start()
     ring_copies[1].wait_recv()
     g_part[down, rear] = g_part[down, rear] + ring_a[1]
     ring_copies[5].start()
-    chunks(lambda k: gather_near(0, k))
     for i in range(PAIRS):
         both = jnp.concatenate([cext[i, :, block(1)], -cext[i + 1, :, block(0)]], axis=0)
         high = both.astype(BF16).astype(F32)
         low = both - high
         ext[i] = jnp.concatenate([high, high, low, low], axis=0).T.astype(BF16)
-    chunks(lambda k: gather_far(0, k))
+    chunks(lambda k: gather(0, k))
     for i in range(2, 6):
         ring_copies[i].wait_recv()
     for q in range(NY):
@@ -442,20 +418,13 @@
 
     chunks(lambda k: coarse(0, k))
 
-    def third(k):
-        finish(1, k, w)
-        start(2, k, w)
-        put_sums(0, k, [product(r, u, k), product(u, w, k)])
-
-    chunks(third)
+    inner(2, image_in(1, w))
+    outer(2, image_in(1, w))
+    chunks(lambda k: put_sums(0, k, [product(r, u, k), product(u, w, k)]))
     send_sums(0)
-
-    def fourth(k):
-        finish(2, k, m0)
-        start(3, k, m0)
-
-    chunks(fourth)
+    inner(3, image_in(2, m0))
     pass_sums(0)
+    outer(3, image_in(2, m0))
     all_coarse(1)
     rz0, den0, alpha0 = [], [], []
     for rz, uw, _ in get_sums(0):
@@ -463,14 +432,17 @@
         den0.append(uw)
         alpha0.append(rz / uw)
 
+    def lowered(k, i):
+        here = (k, block(i))
+        s[here] = w[here]
+        n0[here] = image(3, k, i)
+        w[here] = w[here] - alpha0[k] * n0[here]
+        return w[here]
+
+    inner(4, lowered)
+    outer(4, lowered)
+
     def fifth(k):
-        arrive(3, k)
-        for i in range(PAIRS):
-            here = (k, block(i))
-            s[here] = w[here]
-            n0[here] = image(3, k, i)
-            w[here] = w[here] - alpha0[k] * n0[here]
-        start(4, k, w)
         for i in range(PAIRS):
             here = (k, block(i))
             p[here] = u[here]
@@ -481,14 +453,9 @@
 
     chunks(fifth)
     send_sums(1)
-
-    def sixth(k):
-        finish(4, k, m1)
-        start(5, k, m1, last=True)
-
-    chunks(sixth)
+    inner(5, image_in(4, m1))
     pass_sums(1)
-    chunks(lambda k: gather_near(2, k))
+    outer(5, image_in(4, m1), last=True)
     rz1, den1, alpha1 = [], [], []
     beta1 = []
     for k, (rz, uw, us) in enumerate(get_sums(1)):
@@ -498,7 +465,6 @@
         den1.append(den)
         beta1.append(beta)
         alpha1.append(rz / den)
-    chunks(lambda k: gather_far(2, k))
 
     partial = []
 
@@ -518,7 +484,7 @@
         partial.append([product(r, u, k), product(u, w, k), product(u, s, k), faces])
 
     chunks(seventh)
-    chunks(lambda k: coarse(2, k, last=True))
+    all_coarse(2, last=True)
     for k in range(CHUNKS):
         corner = cown[0, k] - alpha0[k] * cown[1, k] - alpha1[k] * (cown[2, k] + beta1[k] * cown[1, k])
         ru, uw, us, faces = partial[k]
@@ -528,8 +494,10 @@
 
     for i in range(1, NGRP):
         map_copy(i).wait_send()
-    for copy in (count_copy, cpl_right, cpl_left, mate_copy, *ring_copies):
+    for copy in (count_copy, cpl_right, cpl_left, *ring_copies):
         copy.wait_send()
+    for q in range(NY):
+        mate_copy(q).wait_send()
     for t in range(2):
         for i in range(1, NGRP):
             sum_a(t, i).wait_send()
@@ -552,8 +520,10 @@
             back_left(f, k).wait_send()
             if f < 2:
                 back_right(f, k).wait_send()
-            for copy in corner_sends(f, k) + corner_relays(f, k) + corner_forwards(f, k):
-                copy.wait_send()
+            for i in range(NY):
+                corner_copy(f, k, i).wait_send()
+            for i in range(1, NY):
+                corner_forward(f, k, i).wait_send()
 
     chunks(drain)
     for t in range(2):
@@ -582,10 +552,25 @@
         copy.wait()
 
 
-def turn(x_ref, r_ref, x_out, r_out):
-    for source, target in ((x_ref, x_out), (r_ref, r_out)):
+def turn(x_h, r_h, x_out, r_out, taken, given, load_sem, store_sem):
+    def load(side, c):
+        source = (x_h, r_h)[side].at[:, block(c)]
+        return pltpu.make_async_copy(source, taken.at[side, c], load_sem.at[side, c])
+
+    def store(side, c):
+        target = (x_out, r_out)[side].at[0, c]
+        return pltpu.make_async_copy(given.at[side, c], target, store_sem.at[side, c])
+
+    parts = [(side, c) for c in range(SUBS) for side in range(2)]
+    for part in parts:
+        load(*part).start()
+    for side, c in parts:
+        load(side, c).wait()
         for k in range(CHUNKS):
-            target[0, 0, pl.ds(LANES * k, LANES)] = source[k].T
+            given[side, c, pl.ds(LANES * k, LANES)] = taken[side, c, k].T
+        store(side, c).start()
+    for part in parts:
+        store(*part).wait()
 
 
 def local(rhs, counts, solve_panel, dirichlet_panel, coupling, corner_map, coarse_inverse):
@@ -628,9 +613,9 @@
             pltpu.VMEM((3, CHUNKS, OWN + 2 * NC, LANES), F32),
             pltpu.VMEM((3, NGRP, 8, LANES), F32),
             pltpu.VMEM((3, NSUB, 8, LANES), F32),
-            dma((10,)), dma((NGRP,)), dma((NGRP,)), dma((4,)), dma((4,)), dma((CHUNKS,)), dma((CHUNKS,)),
+            dma((10,)), dma((NGRP,)), dma((NGRP,)), dma((7,)), dma((7,)), dma((CHUNKS,)), dma((CHUNKS,)),
             dma((6, 2, CHUNKS)), dma((6, 2, CHUNKS)), dma((3, 2, CHUNKS)), dma((3, 2, CHUNKS)),
-            dma((3, CHUNKS, 9)), dma((3, CHUNKS, 9)),
+            dma((3, CHUNKS, 7)), dma((3, CHUNKS, 7)),
             dma((3, NGRP)), dma((3, NGRP)), dma((3, NSUB)), dma((3, NSUB)), dma((6,)), dma((6,)),
         ],
         compiler_params=pltpu.CompilerParams(
@@ -638,14 +623,16 @@
         ),
     )(rhs, counts, solve_panel, dirichlet_panel, coupling, corner_map, coarse_inverse)
     out = jax.ShapeDtypeStruct(rhs.shape, F32)
-    taken = pl.BlockSpec((CHUNKS, H, LANES), lambda c: (0, c, 0))
-    given = pl.BlockSpec((1, 1, CHUNKS * LANES, H), lambda c: (0, c, 0, 0))
     return pl.pallas_call(
         turn,
         out_shape=(out, out),
-        grid=(SUBS,),
-        in_specs=[taken, taken],
-        out_specs=(given, given),
+        in_specs=[anywhere, anywhere],
+        out_specs=(anywhere, anywhere),
+        scratch_shapes=[
+            pltpu.VMEM((2, SUBS, CHUNKS, H, LANES), F32),
+            pltpu.VMEM((2, SUBS, CHUNKS * LANES, H), F32),
+            dma((2, SUBS)), dma((2, SUBS)),
+        ],
     )(x_turned, r_turned)
 
 

time: 112 us -> 105 us (0.938)
  Pallas kernels: 111 us -> 104 us
    pallas_call x1, Pallas kernels: 107 us -> 101 us  [local(): pl.pallas_call(kernel, out_shape=(shape, shape), in_specs=[anywhere, pl.B...]
where the time goes in v3:
time: 105 us
  Pallas kernels  104 us (99%)
    pallas_call x1, Pallas kernels, local(): pl.pallas_call(kernel, out_shape=(shape, shape), in_specs=[anywhere, pl.B...  101 us
    pallas_call x1, Pallas kernels, local(): pl.pallas_call(turn, out_shape=(out, out), in_specs=[anywhere, anywhere],...  2.88 us

profile of v3, /device:TPU:1, one launch (start us, length us, event | category | flops | bytes accessed | tf_op | source)
XLA Modules:
  0.0 105.0 jit_solution(8839883496315294784)
XLA Ops:
  0.6 101.3 %shard_map.86 = (f32[2,1024,128]{2,1,0:T(8,128)}, f32[2,1024,128]{2,1,0:T(8,128)}) custom-call(f32[1,4,256,256]{3,2,1,0:T(8,128)} %rhs_h.1, s32[1,4]{1,0:T(1,128)} %counts_s.1, bf16[1,4,512,512]{3,2,1,0:T(8,128)(2,1)} %solve_h.1, bf16[1,4,512,512]{3,2,1,0:T(8,128)(2,1)} %dirichlet_h.1, f32[1,4,32,512]{3,2,1,0:T(8,128)} %coupling_h.1, s32[1,4,32]{2,1,0:T(4,128)} %map_h.1, ...), custom_call_target="tpu_custom_call" | custom-call | tf_op jit(solution)/shard_map/pallas_call | solution.py:581
  101.9 2.9 %shard_map.87 = (f32[1,4,256,256]{3,2,1,0:T(8,128)}, f32[1,4,256,256]{3,2,1,0:T(8,128)}) custom-call(f32[2,1024,128]{2,1,0:T(8,128)} %get-tuple-element.4.x_h, f32[2,1024,128]{2,1,0:T(8,128)} %get-tuple-element.5.r_h), custom_call_target="tpu_custom_call" | custom-call | tf_op jit(solution)/shard_map/pallas_call | solution.py:626

commit v4 on v3

--- a/solution.py
+++ b/solution.py
@@ -98,18 +98,15 @@
         part = a_part.at[core if mine else 1 - core, q]
         return remote(part, part, misc_send.at[3 + q], misc_recv.at[3 + q], to_mate)
 
-    def ring(i, source, target, device):
-        return remote(source, target, ring_send.at[i], ring_recv.at[i], device)
-
-    front, rear = pl.ds(0, 2), pl.ds(2, 2)
-    ring_copies = [
-        ring(0, g_part.at[far, front], ring_a.at[0], to_up),
-        ring(1, g_part.at[far, rear], ring_a.at[1], to_down),
-        ring(2, g_part.at[up, rear], ring_b.at[0, rear], to_up),
-        ring(3, g_part.at[down, front], ring_b.at[1, front], to_down),
-        ring(4, g_part.at[up, front], ring_b.at[0, front], to_up),
-        ring(5, g_part.at[down, rear], ring_b.at[1, rear], to_down),
-    ]
+    def ring(stage, q):
+        upward = (q < 2) == (stage != 1)
+        if stage == 0:
+            source, target = g_part.at[far, q], ring_a.at[q]
+        else:
+            source, target = g_part.at[up if upward else down, q], ring_b.at[0 if upward else 1, q]
+        return remote(
+            source, target, ring_send.at[stage, q], ring_recv.at[stage, q], to_up if upward else to_down
+        )
 
     def halo_copy(k):
         part = pl.ds(LANES * k, LANES)
@@ -198,8 +195,8 @@
             apply_panel(op, k, 1)
             apply_panel(op, k, 2)
 
-    def outer(op, value, last=False):
-        for k in range(CHUNKS):
+    def outer(op, value, last=False, parts=range(CHUNKS)):
+        for k in parts:
             if op > 0:
                 arrive(op - 1, k)
             if op >= 2:
@@ -348,24 +345,37 @@
                 onehot[pl.ds(256 * t, 256), pl.ds(LANES * c, LANES)] = hit.astype(F32).astype(BF16)
 
     slots = (onehot_a, onehot_b)
-    fill(onehot_a, 0)
-    for q in range(NY):
-        if q + 1 < NY:
-            fill(slots[(q + 1) % 2], q + 1)
-        both = jnp.dot(cis[...], slots[q % 2][...], preferred_element_type=F32)
+    order = (0, 2, 1, 3)
+
+    def columns(n):
+        q, onehot = order[n], slots[n % 2]
+        both = jnp.dot(cis[...], onehot[...], preferred_element_type=F32)
         a_part[core, q] = both[:256] + both[256:]
         mate_copy(q).start()
 
-    count_copy.wait_recv()
-    mask[0] = (rows < cnt[1, pl.ds(0, 1)]).astype(F32)
-    outer(0, residual)
-
-    for q in range(NY):
+    def rows_of(n):
+        q = order[n]
         mate_copy(q, False).wait_recv()
         for c in range(2):
             high, low = split(a_part[c, q])
             a_split[q, block(c), pl.ds(0, 256)] = high
             a_split[q, block(c), pl.ds(256, 256)] = low
+        both = jnp.dot(rowhot[...], a_split[q], preferred_element_type=F32)
+        both = both[:, :256] + both[:, 256:]
+        for chip in range(NY):
+            g_part[chip, q] = both[LANES * chip : LANES * (chip + 1)]
+        ring(0, q).start()
+        ring(1, q).start()
+
+    def add_row(q):
+        ring(0, q).wait_recv()
+        there = (up if q < 2 else down, q)
+        g_part[there] = g_part[there] + ring_a[q]
+        ring(2, q).start()
+
+    fill(onehot_a, order[0])
+    fill(onehot_b, order[1])
+    columns(0)
     lane = lax.broadcasted_iota(I32, (LANES, LANES), 1).astype(F32)
     base = (2 * 256 * y).astype(F32)
     for q in range(NY):
@@ -374,13 +384,19 @@
             rowhot[pl.ds(LANES * q, LANES), pl.ds(LANES * t, LANES)] = (
                 wanted == lane + (base + 128.0 * t)
             ).astype(F32).astype(BF16)
-    for q in range(NY):
-        both = jnp.dot(rowhot[...], a_split[q], preferred_element_type=F32)
-        both = both[:, :256] + both[:, 256:]
-        for chip in range(NY):
-            g_part[chip, q] = both[LANES * chip : LANES * (chip + 1)]
-    for i in range(4):
-        ring_copies[i].start()
+    fill(onehot_a, order[2])
+    columns(1)
+    rows_of(0)
+    fill(onehot_b, order[3])
+    columns(2)
+    count_copy.wait_recv()
+    mask[0] = (rows < cnt[1, pl.ds(0, 1)]).astype(F32)
+    outer(0, residual, parts=(0,))
+    rows_of(1)
+    columns(3)
+    outer(0, residual, parts=(1,))
+    rows_of(2)
+    rows_of(3)
 
     loads[5].wait()
     loads[4].wait()
@@ -396,22 +412,21 @@
             sc[j, pl.ds(PS + NC, NC), block(half)] = low
 
     inner(1, image_in(0, u))
-    outer(1, image_in(0, u))
-    ring_copies[0].wait_recv()
-    g_part[up, front] = g_part[up, front] + ring_a[0]
-    ring_copies[4].start()
-    ring_copies[1].wait_recv()
-    g_part[down, rear] = g_part[down, rear] + ring_a[1]
-    ring_copies[5].start()
+    add_row(0)
+    add_row(2)
+    outer(1, image_in(0, u), parts=(0,))
+    add_row(1)
+    add_row(3)
+    outer(1, image_in(0, u), parts=(1,))
     for i in range(PAIRS):
         both = jnp.concatenate([cext[i, :, block(1)], -cext[i + 1, :, block(0)]], axis=0)
         high = both.astype(BF16).astype(F32)
         low = both - high
         ext[i] = jnp.concatenate([high, high, low, low], axis=0).T.astype(BF16)
     chunks(lambda k: gather(0, k))
-    for i in range(2, 6):
-        ring_copies[i].wait_recv()
     for q in range(NY):
+        ring(1, q).wait_recv()
+        ring(2, q).wait_recv()
         high, low = split(g_part[y, q] + ring_b[0, q] + ring_b[1, q])
         gs[pl.ds(0, OWN), pl.ds(256 * q, 256)] = high
         gs[pl.ds(OWN, OWN), pl.ds(256 * q, 256)] = low
@@ -494,10 +509,12 @@
 
     for i in range(1, NGRP):
         map_copy(i).wait_send()
-    for copy in (count_copy, cpl_right, cpl_left, *ring_copies):
+    for copy in (count_copy, cpl_right, cpl_left):
         copy.wait_send()
     for q in range(NY):
         mate_copy(q).wait_send()
+        for stage in range(3):
+            ring(stage, q).wait_send()
     for t in range(2):
         for i in range(1, NGRP):
             sum_a(t, i).wait_send()
@@ -598,7 +615,7 @@
             pltpu.VMEM((2, NY, 256, 256), F32),
             pltpu.VMEM((NY, 512, 512), BF16),
             pltpu.VMEM((NY, NY, OWN, 256), F32),
-            pltpu.VMEM((2, 2, OWN, 256), F32),
+            pltpu.VMEM((NY, OWN, 256), F32),
             pltpu.VMEM((2, NY, OWN, 256), F32),
             pltpu.VMEM((2 * OWN, NGRP * OWN), BF16),
             pltpu.VMEM((PAIRS, H, 8 * NC), BF16),
@@ -616,7 +633,7 @@
             dma((10,)), dma((NGRP,)), dma((NGRP,)), dma((7,)), dma((7,)), dma((CHUNKS,)), dma((CHUNKS,)),
             dma((6, 2, CHUNKS)), dma((6, 2, CHUNKS)), dma((3, 2, CHUNKS)), dma((3, 2, CHUNKS)),
             dma((3, CHUNKS, 7)), dma((3, CHUNKS, 7)),
-            dma((3, NGRP)), dma((3, NGRP)), dma((3, NSUB)), dma((3, NSUB)), dma((6,)), dma((6,)),
+            dma((3, NGRP)), dma((3, NGRP)), dma((3, NSUB)), dma((3, NSUB)), dma((3, NY)), dma((3, NY)),
         ],
         compiler_params=pltpu.CompilerParams(
             collective_id=0, has_side_effects=True, vmem_limit_bytes=66_000_000

time: 105 us -> 100 us (0.952)
  Pallas kernels: 104 us -> 99.1 us
    pallas_call x1, Pallas kernels: 101 us -> 96.2 us  [local(): pl.pallas_call(kernel, out_shape=(shape, shape), in_specs=[anywhere, pl.B...]
where the time goes in v4:
time: 100 us; the launch traced here: 99.9 us
  Pallas kernels  99.1 us (99%)
    pallas_call x1, Pallas kernels, local(): pl.pallas_call(kernel, out_shape=(shape, shape), in_specs=[anywhere, pl.B...  96.2 us
    pallas_call x1, Pallas kernels, local(): pl.pallas_call(turn, out_shape=(out, out), in_specs=[anywhere, anywhere],...  2.88 us

profile of v4, /device:TPU:1, one launch (start us, length us, event | category | flops | bytes accessed | tf_op | source)
XLA Modules:
  0.0 99.9 jit_solution(15366452118026087946)
XLA Ops:
  0.6 96.2 %shard_map.86 = (f32[2,1024,128]{2,1,0:T(8,128)}, f32[2,1024,128]{2,1,0:T(8,128)}) custom-call(f32[1,4,256,256]{3,2,1,0:T(8,128)} %rhs_h.1, s32[1,4]{1,0:T(1,128)} %counts_s.1, bf16[1,4,512,512]{3,2,1,0:T(8,128)(2,1)} %solve_h.1, bf16[1,4,512,512]{3,2,1,0:T(8,128)(2,1)} %dirichlet_h.1, f32[1,4,32,512]{3,2,1,0:T(8,128)} %coupling_h.1, s32[1,4,32]{2,1,0:T(4,128)} %map_h.1, ...), custom_call_target="tpu_custom_call" | custom-call | tf_op jit(solution)/shard_map/pallas_call | solution.py:598
  96.9 2.9 %shard_map.87 = (f32[1,4,256,256]{3,2,1,0:T(8,128)}, f32[1,4,256,256]{3,2,1,0:T(8,128)}) custom-call(f32[2,1024,128]{2,1,0:T(8,128)} %get-tuple-element.4.x_h, f32[2,1024,128]{2,1,0:T(8,128)} %get-tuple-element.5.r_h), custom_call_target="tpu_custom_call" | custom-call | tf_op jit(solution)/shard_map/pallas_call | solution.py:643

commit v5 on v4

--- a/solution.py
+++ b/solution.py
@@ -171,17 +171,25 @@
         return remote(there, there, rb_send.at[t, i], rb_recv.at[t, i], to_right)
 
 
+    def panel_rows(op, k, j, first, count):
+        panel = (sc if op % 2 == 1 else dm)[j, pl.ds(first, count)]
+        both = jnp.dot(panel, vs[k, pl.ds(H * j, PS), :], preferred_element_type=F32)
+        return both[:, :LANES] + both[:, LANES:]
+
+    def put_corner(op, k, j, both):
+        f = op // 2
+        values = both[:NC] + both[NC:]
+        cown[f, k, pl.ds(NC * j, NC)] = values
+        corners[f, k, grp, pl.ds(NC * j, NC)] = values
+
     def apply_panel(op, k, j):
-        solve = op % 2 == 1
-        faces = vs[k, pl.ds(H * j, PS), :]
-        both = jnp.dot((sc if solve else dm)[j], faces, preferred_element_type=F32)
-        both = both[:, :LANES] + both[:, LANES:]
+        both = panel_rows(op, k, j, 0, PS + (2 * NC if op % 2 == 1 else 0))
         wb[op % 2, k, j] = both[:PS]
-        if solve:
-            f = op // 2
-            values = both[PS : PS + NC] + both[PS + NC :]
-            cown[f, k, pl.ds(NC * j, NC)] = values
-            corners[f, k, grp, pl.ds(NC * j, NC)] = values
+        if op % 2 == 1:
+            put_corner(op, k, j, both[PS:])
+
+    def apply_half(op, k, j, half):
+        wb[op % 2, k, j, block(half)] = panel_rows(op, k, j, H * half, H)
 
     def put_faces(k, pairs, value):
         for i in pairs:
@@ -203,14 +211,18 @@
                 face_left(op - 2, k).wait_send()
                 face_right(op - 2, k).wait_send()
             put_faces(k, (0, SUBS), value)
-            apply_panel(op, k, 0)
-            face_left(op, k).start()
-            apply_panel(op, k, SUBS - 1)
             if op % 2 == 1:
+                for j in (0, SUBS - 1):
+                    put_corner(op, k, j, panel_rows(op, k, j, PS, 2 * NC))
                 for i in (2, 1, 3, 0):
                     corner_copy(op // 2, k, i).start()
+            apply_half(op, k, 0, 0)
+            face_left(op, k).start()
+            apply_half(op, k, SUBS - 1, 1)
             if not last:
                 face_right(op, k).start()
+            apply_half(op, k, 0, 1)
+            apply_half(op, k, SUBS - 1, 0)
 
     def gather(f, k):
         for i in (1, 3, 2):

time: 100 us -> 99.4 us (level)
  no operation moved by 1% of the time
where the time goes in v5:
time: 99.4 us; the launch traced here: 99.2 us
  Pallas kernels  98.4 us (99%)
    pallas_call x1, Pallas kernels, local(): pl.pallas_call(kernel, out_shape=(shape, shape), in_specs=[anywhere, pl.B...  95.6 us
    pallas_call x1, Pallas kernels, local(): pl.pallas_call(turn, out_shape=(out, out), in_specs=[anywhere, anywhere],...  2.88 us

profile of v5, /device:TPU:1, one launch (start us, length us, event | category | flops | bytes accessed | tf_op | source)
XLA Modules:
  0.0 99.2 jit_solution(11432481827721426309)
XLA Ops:
  0.6 95.6 %shard_map.86 = (f32[2,1024,128]{2,1,0:T(8,128)}, f32[2,1024,128]{2,1,0:T(8,128)}) custom-call(f32[1,4,256,256]{3,2,1,0:T(8,128)} %rhs_h.1, s32[1,4]{1,0:T(1,128)} %counts_s.1, bf16[1,4,512,512]{3,2,1,0:T(8,128)(2,1)} %solve_h.1, bf16[1,4,512,512]{3,2,1,0:T(8,128)(2,1)} %dirichlet_h.1, f32[1,4,32,512]{3,2,1,0:T(8,128)} %coupling_h.1, s32[1,4,32]{2,1,0:T(4,128)} %map_h.1, ...), custom_call_target="tpu_custom_call" | custom-call | tf_op jit(solution)/shard_map/pallas_call | solution.py:610
  96.2 2.9 %shard_map.87 = (f32[1,4,256,256]{3,2,1,0:T(8,128)}, f32[1,4,256,256]{3,2,1,0:T(8,128)}) custom-call(f32[2,1024,128]{2,1,0:T(8,128)} %get-tuple-element.4.x_h, f32[2,1024,128]{2,1,0:T(8,128)} %get-tuple-element.5.r_h), custom_call_target="tpu_custom_call" | custom-call | tf_op jit(solution)/shard_map/pallas_call | solution.py:655

commit v6 on v5

--- a/solution.py
+++ b/solution.py
@@ -47,9 +47,10 @@
 def kernel(
     rhs_h, counts_s, solve_h, dirichlet_h, coupling_h, map_h, coarse_h, x_h, res_h,
     rhs_v, sc, dm, cext, ci, cis, cmt, cnt, onehot_a, onehot_b, rowhot, a_part, a_split, g_part, ring_a, ring_b,
-    gs, ext, mask, r, u, w, m0, n0, m1, p, s, x, vs, wb, from_left, from_right, corners, cown, bext, red_a, red_b,
+    gs, ps, shared, shares, ext, mask, r, u, w, m0, n0, m1, p, s, x, vs, wb, from_left, from_right, corners, cown, bext, red_a, red_b,
     load_sem, cm_send, cm_recv, misc_send, misc_recv, halo_send, halo_recv, ex_send, ex_recv,
     bk_send, bk_recv, ag_send, ag_recv, ra_send, ra_recv, rb_send, rb_recv, ring_send, ring_recv,
+    share_send, share_recv,
 ):
     sub, grp = lax.axis_index("sub"), lax.axis_index("grp")
     right, left = lax.rem(sub + 1, NSUB), lax.rem(sub + NSUB - 1, NSUB)
@@ -229,14 +230,48 @@
             corner_arrival(f, k, i).wait_recv()
             corner_forward(f, k, i).start()
 
-    def coarse(f, k, last=False):
+    def gathered(f, k):
         corner_arrival(f, k, 0).wait_recv()
         for i in range(1, NY):
             corner_forward(f, k, i, False).wait_recv()
         high, low = split(corners[f, k].reshape(NGRP * OWN, LANES))
-        both = jnp.dot(gs[...], jnp.concatenate([high, low], axis=1), preferred_element_type=F32)
+        return jnp.concatenate([high, low], axis=1)
+
+    def quadrants(rows, values):
+        both = jnp.dot(rows, values, preferred_element_type=F32)
         both = both[:, :LANES] + both[:, LANES:]
-        bext[f, k, pl.ds(NC, OWN)] = both[:OWN] + both[OWN:]
+        return both[:OWN] + both[OWN:]
+
+    def share_copy(k, step):
+        chip = lax.rem(y + step, NY)
+        return remote(
+            shared.at[k, chip], shares.at[k, y], share_send.at[k, step], share_recv.at[k, step],
+            {"grp": 2 * chip + core},
+        )
+
+    def share_arrival(k, step):
+        there = shares.at[k, lax.rem(y + NY - step, NY)]
+        return remote(there, there, share_send.at[k, step], share_recv.at[k, step], to_mate)
+
+    def scatter(k):
+        values = gathered(0, k)
+        for step in (2, 1, 3, 0):
+            chip = lax.rem(y + step, NY)
+            shared[k, chip] = quadrants(ps[chip], values)
+            if step:
+                share_copy(k, step).start()
+
+    def collect(k):
+        total = shared[k, y]
+        for step in range(1, NY):
+            share_arrival(k, step).wait_recv()
+            total = total + shares[k, lax.rem(y + NY - step, NY)]
+        bext[0, k, pl.ds(NC, OWN)] = total
+        back_left(0, k).start()
+        back_right(0, k).start()
+
+    def coarse(f, k, last=False):
+        bext[f, k, pl.ds(NC, OWN)] = quadrants(gs[...], gathered(f, k))
         back_left(f, k).start()
         if not last:
             back_right(f, k).start()
@@ -375,9 +410,11 @@
         both = jnp.dot(rowhot[...], a_split[q], preferred_element_type=F32)
         both = both[:, :256] + both[:, 256:]
         for chip in range(NY):
-            g_part[chip, q] = both[LANES * chip : LANES * (chip + 1)]
-        ring(0, q).start()
-        ring(1, q).start()
+            part = both[LANES * chip : LANES * (chip + 1)]
+            g_part[chip, q] = part
+            high, low = split(part)
+            ps[chip, pl.ds(0, OWN), pl.ds(256 * q, 256)] = high
+            ps[chip, pl.ds(OWN, OWN), pl.ds(256 * q, 256)] = low
 
     def add_row(q):
         ring(0, q).wait_recv()
@@ -424,34 +461,34 @@
             sc[j, pl.ds(PS + NC, NC), block(half)] = low
 
     inner(1, image_in(0, u))
-    add_row(0)
-    add_row(2)
-    outer(1, image_in(0, u), parts=(0,))
-    add_row(1)
-    add_row(3)
-    outer(1, image_in(0, u), parts=(1,))
+    outer(1, image_in(0, u))
     for i in range(PAIRS):
         both = jnp.concatenate([cext[i, :, block(1)], -cext[i + 1, :, block(0)]], axis=0)
         high = both.astype(BF16).astype(F32)
         low = both - high
         ext[i] = jnp.concatenate([high, high, low, low], axis=0).T.astype(BF16)
     chunks(lambda k: gather(0, k))
+    chunks(scatter)
+    for q in order:
+        ring(0, q).start()
+        ring(1, q).start()
+    chunks(collect)
+
+    inner(2, image_in(1, w))
+    outer(2, image_in(1, w))
+    chunks(lambda k: put_sums(0, k, [product(r, u, k), product(u, w, k)]))
+    send_sums(0)
+    inner(3, image_in(2, m0))
+    pass_sums(0)
+    for q in order:
+        add_row(q)
+    outer(3, image_in(2, m0))
     for q in range(NY):
         ring(1, q).wait_recv()
         ring(2, q).wait_recv()
         high, low = split(g_part[y, q] + ring_b[0, q] + ring_b[1, q])
         gs[pl.ds(0, OWN), pl.ds(256 * q, 256)] = high
         gs[pl.ds(OWN, OWN), pl.ds(256 * q, 256)] = low
-
-    chunks(lambda k: coarse(0, k))
-
-    inner(2, image_in(1, w))
-    outer(2, image_in(1, w))
-    chunks(lambda k: put_sums(0, k, [product(r, u, k), product(u, w, k)]))
-    send_sums(0)
-    inner(3, image_in(2, m0))
-    pass_sums(0)
-    outer(3, image_in(2, m0))
     all_coarse(1)
     rz0, den0, alpha0 = [], [], []
     for rz, uw, _ in get_sums(0):
@@ -542,6 +579,8 @@
 
     def drain(k):
         halo_copy(k).wait_send()
+        for step in range(1, NY):
+            share_copy(k, step).wait_send()
         face_left(4, k).wait_send()
         face_right(4, k).wait_send()
         face_left(5, k).wait_send()
@@ -630,6 +669,9 @@
             pltpu.VMEM((NY, OWN, 256), F32),
             pltpu.VMEM((2, NY, OWN, 256), F32),
             pltpu.VMEM((2 * OWN, NGRP * OWN), BF16),
+            pltpu.VMEM((NY, 2 * OWN, NGRP * OWN), BF16),
+            pltpu.VMEM((CHUNKS, NY, OWN, LANES), F32),
+            pltpu.VMEM((CHUNKS, NY, OWN, LANES), F32),
             pltpu.VMEM((PAIRS, H, 8 * NC), BF16),
             pltpu.VMEM((PAIRS, H, LANES), F32),
             vector, vector, vector, vector, vector, vector, vector, vector, vector,
@@ -646,6 +688,7 @@
             dma((6, 2, CHUNKS)), dma((6, 2, CHUNKS)), dma((3, 2, CHUNKS)), dma((3, 2, CHUNKS)),
             dma((3, CHUNKS, 7)), dma((3, CHUNKS, 7)),
             dma((3, NGRP)), dma((3, NGRP)), dma((3, NSUB)), dma((3, NSUB)), dma((3, NY)), dma((3, NY)),
+            dma((CHUNKS, NY)), dma((CHUNKS, NY)),
         ],
         compiler_params=pltpu.CompilerParams(
             collective_id=0, has_side_effects=True, vmem_limit_bytes=66_000_000

time: 99.4 us -> 104 us (1.046)
  Pallas kernels: 98.4 us -> 103 us
    pallas_call x1, Pallas kernels: 95.6 us -> 100 us  [local(): pl.pallas_call(kernel, out_shape=(shape, shape), in_specs=[anywhere, pl.B...]
where the time goes in v6:
time: 104 us
  Pallas kernels  103 us (99%)
    pallas_call x1, Pallas kernels, local(): pl.pallas_call(kernel, out_shape=(shape, shape), in_specs=[anywhere, pl.B...  100 us
    pallas_call x1, Pallas kernels, local(): pl.pallas_call(turn, out_shape=(out, out), in_specs=[anywhere, anywhere],...  2.88 us

profile of v6, /device:TPU:1, one launch (start us, length us, event | category | flops | bytes accessed | tf_op | source)
XLA Modules:
  0.0 103.7 jit_solution(12315357212265870676)
XLA Ops:
  0.6 100.0 %shard_map.86 = (f32[2,1024,128]{2,1,0:T(8,128)}, f32[2,1024,128]{2,1,0:T(8,128)}) custom-call(f32[1,4,256,256]{3,2,1,0:T(8,128)} %rhs_h.1, s32[1,4]{1,0:T(1,128)} %counts_s.1, bf16[1,4,512,512]{3,2,1,0:T(8,128)(2,1)} %solve_h.1, bf16[1,4,512,512]{3,2,1,0:T(8,128)(2,1)} %dirichlet_h.1, f32[1,4,32,512]{3,2,1,0:T(8,128)} %coupling_h.1, s32[1,4,32]{2,1,0:T(4,128)} %map_h.1, ...), custom_call_target="tpu_custom_call" | custom-call | tf_op jit(solution)/shard_map/pallas_call | solution.py:649
  100.6 2.9 %shard_map.87 = (f32[1,4,256,256]{3,2,1,0:T(8,128)}, f32[1,4,256,256]{3,2,1,0:T(8,128)}) custom-call(f32[2,1024,128]{2,1,0:T(8,128)} %get-tuple-element.4.x_h, f32[2,1024,128]{2,1,0:T(8,128)} %get-tuple-element.5.r_h), custom_call_target="tpu_custom_call" | custom-call | tf_op jit(solution)/shard_map/pallas_call | solution.py:698

commit v7 on v5

--- a/solution.py
+++ b/solution.py
@@ -426,10 +426,9 @@
     inner(1, image_in(0, u))
     add_row(0)
     add_row(2)
-    outer(1, image_in(0, u), parts=(0,))
+    outer(1, image_in(0, u))
     add_row(1)
     add_row(3)
-    outer(1, image_in(0, u), parts=(1,))
     for i in range(PAIRS):
         both = jnp.concatenate([cext[i, :, block(1)], -cext[i + 1, :, block(0)]], axis=0)
         high = both.astype(BF16).astype(F32)

time: 99.4 us -> 99.3 us (level)
  no operation moved by 1% of the time
where the time goes in v7:
time: 99.3 us; the launch traced here: 99.2 us
  Pallas kernels  98.4 us (99%)
    pallas_call x1, Pallas kernels, local(): pl.pallas_call(kernel, out_shape=(shape, shape), in_specs=[anywhere, pl.B...  95.5 us
    pallas_call x1, Pallas kernels, local(): pl.pallas_call(turn, out_shape=(out, out), in_specs=[anywhere, anywhere],...  2.88 us

profile of v7, /device:TPU:1, one launch (start us, length us, event | category | flops | bytes accessed | tf_op | source)
XLA Modules:
  0.0 99.2 jit_solution(3576489711576966289)
XLA Ops:
  0.6 95.5 %shard_map.86 = (f32[2,1024,128]{2,1,0:T(8,128)}, f32[2,1024,128]{2,1,0:T(8,128)}) custom-call(f32[1,4,256,256]{3,2,1,0:T(8,128)} %rhs_h.1, s32[1,4]{1,0:T(1,128)} %counts_s.1, bf16[1,4,512,512]{3,2,1,0:T(8,128)(2,1)} %solve_h.1, bf16[1,4,512,512]{3,2,1,0:T(8,128)(2,1)} %dirichlet_h.1, f32[1,4,32,512]{3,2,1,0:T(8,128)} %coupling_h.1, s32[1,4,32]{2,1,0:T(4,128)} %map_h.1, ...), custom_call_target="tpu_custom_call" | custom-call | tf_op jit(solution)/shard_map/pallas_call | solution.py:609
  96.1 2.9 %shard_map.87 = (f32[1,4,256,256]{3,2,1,0:T(8,128)}, f32[1,4,256,256]{3,2,1,0:T(8,128)}) custom-call(f32[2,1024,128]{2,1,0:T(8,128)} %get-tuple-element.4.x_h, f32[2,1024,128]{2,1,0:T(8,128)} %get-tuple-element.5.r_h), custom_call_target="tpu_custom_call" | custom-call | tf_op jit(solution)/shard_map/pallas_call | solution.py:654
